TPU v7x, 32 devices: a whole 2x2x4 slice. The times are simulated.
32 devices in a mesh: row: 8 (over z, core), col: 4 (over y, x).
Axes of the slice: x: 2, y: 2, z: 4, core: 2. Of those that a mesh axis runs over, the one named last changes fastest.
Arguments:
- queries: bfloat16 [512, 8192], P('col', 'row'), may hold values from -8 to 8
- cache_keys: bfloat16 [8, 32768, 128], P(None, ('row', 'col')), may hold values from -8 to 8
- cache_values: bfloat16 [8, 32768, 128], P(None, ('row', 'col')), may hold values from -6 to 6
- stretch_keys: bfloat16 [8, 512, 128], P(None, 'col'), may hold values from -8 to 8
- stretch_values: bfloat16 [8, 512, 128], P(None, 'col'), may hold values from -6 to 6
- block_lists: int32 [4, 8, 16], replicated, may hold values from 0 to 255, as said below
- out_weight: bfloat16 [8192, 8192], P('row', 'col'), may hold values from -0.5 to 0.5
- residual: bfloat16 [512, 8192], P('row', 'col'), may hold values from -6 to 6
- norm_gain: bfloat16 [8192], P('col'), may hold values from 0.25 to 1.75
- gate_weight: bfloat16 [8192, 28672], P('col', 'row'), may hold values from -0.0625 to 0.0625
- up_weight: bfloat16 [8192, 28672], P('col', 'row'), may hold values from -0.0625 to 0.0625
- down_weight: bfloat16 [28672, 8192], P('row', 'col'), may hold values from -0.03125 to 0.03125
Outputs:
- layer_out: bfloat16 [512, 8192], P('row', 'col')
Inputs may be any that keep to these rules, and one draw needn't show every extreme that they name: `block_lists`: each list names 16 different cache blocks; device k of row+col holds cache blocks k * (8) to (k + 1) * 8 - 1, and no two blocks of one list lie on the same device. Every list holds block 0 and block 255.
All inputs are finite; a program needn't handle non-finite values.
Results may differ from a plain program's by a relative error of at most 0.0085.
Values may be sent and summed in bfloat16 or wider, within the bound.
A program may use at most 128 MiB of HBM per device.

v0:
```python
import math

import jax
import jax.numpy as jnp
from jax import lax
from jax.sharding import PartitionSpec as P

D = 8192
KV_HEADS = 8
HEAD_DIM = 128
BLK = 128
GROUP = 8


def local(
    queries,
    cache_keys,
    cache_values,
    stretch_keys,
    stretch_values,
    block_lists,
    out_weight,
    residual,
    norm_gain,
    gate_weight,
    up_weight,
    down_weight,
):
    row_count = lax.axis_size("row")
    col_count = lax.axis_size("col")
    row_index = lax.axis_index("row")
    col_index = lax.axis_index("col")
    device_count = row_count * col_count
    my_index = row_index * col_count + col_index
    local_blocks = cache_keys.shape[1] // BLK
    heads_here = queries.shape[1] // HEAD_DIM
    list_length = block_lists.shape[2]
    my_group = row_index * heads_here // GROUP
    scaling = 1.0 / math.sqrt(HEAD_DIM)
    targets = jnp.arange(device_count, dtype=jnp.int32)
    target_group = targets // col_count * heads_here // GROUP
    target_lists = block_lists[targets % col_count, target_group]
    holders = target_lists // local_blocks
    matched = holders == my_index
    found_any = jnp.any(matched, axis=1)
    within = jnp.sum(jnp.where(matched, target_lists % local_blocks, 0), axis=1)
    source_rows = target_group * local_blocks + within
    flat_keys = cache_keys.reshape(KV_HEADS * local_blocks, BLK, HEAD_DIM)
    flat_values = cache_values.reshape(KV_HEADS * local_blocks, BLK, HEAD_DIM)
    outgoing = jnp.concatenate([flat_keys[source_rows], flat_values[source_rows]], axis=2)
    outgoing = jnp.where(found_any[:, None, None], outgoing, jnp.zeros_like(outgoing))
    arrived = lax.all_to_all(outgoing, ("row", "col"), split_axis=0, concat_axis=0, tiled=True)
    my_list = block_lists[col_index, my_group]
    fetched = arrived[my_list // local_blocks].reshape(list_length * BLK, 2 * HEAD_DIM)
    far_keys = fetched[:, :HEAD_DIM]
    far_values = fetched[:, HEAD_DIM:]
    query_rows = queries.reshape(BLK * heads_here, HEAD_DIM)
    far_scores = jnp.dot(query_rows, far_keys.T, preferred_element_type=jnp.float32) * scaling
    run_max = jnp.max(far_scores, axis=1)
    far_exp = jnp.exp(far_scores - run_max[:, None])
    run_sum = jnp.sum(far_exp, axis=1)
    run_acc = jnp.dot(far_exp.astype(jnp.bfloat16), far_values, preferred_element_type=jnp.float32)
    query_pos = col_index * BLK + jnp.arange(BLK * heads_here, dtype=jnp.int32) // heads_here
    own_keys = lax.dynamic_index_in_dim(stretch_keys, my_group, 0, keepdims=False)
    own_values = lax.dynamic_index_in_dim(stretch_values, my_group, 0, keepdims=False)
    piece_keys = lax.all_gather(own_keys, "col", axis=0, tiled=True)
    piece_values = lax.all_gather(own_values, "col", axis=0, tiled=True)
    scores = jnp.dot(query_rows, piece_keys.T, preferred_element_type=jnp.float32) * scaling
    key_pos = jnp.arange(piece_keys.shape[0], dtype=jnp.int32)
    allowed = key_pos[None, :] <= query_pos[:, None]
    scores = jnp.where(allowed, scores, -1e30)
    new_max = jnp.maximum(run_max, jnp.max(scores, axis=1))
    decays = jnp.exp(run_max - new_max)
    weights = jnp.where(allowed, jnp.exp(scores - new_max[:, None]), 0.0)
    new_sum = run_sum * decays + jnp.sum(weights, axis=1)
    new_acc = run_acc * decays[:, None] + jnp.dot(
        weights.astype(jnp.bfloat16), piece_values, preferred_element_type=jnp.float32
    )
    attended = (new_acc / new_sum[:, None]).astype(jnp.bfloat16).reshape(BLK, heads_here * HEAD_DIM)
    all_attended = lax.all_gather(attended, "col", axis=0, tiled=True)
    projected = lax.psum_scatter(
        jnp.dot(all_attended, out_weight, preferred_element_type=jnp.float32),
        "row",
        scatter_dimension=0,
        tiled=True,
    )
    stream = residual.astype(jnp.float32) + projected
    squares = lax.psum(jnp.sum(stream * stream, axis=1), "col")
    normed = (
        stream * lax.rsqrt(squares / D + 1e-05)[:, None] * norm_gain.astype(jnp.float32)
    ).astype(jnp.bfloat16)
    block_piece = lax.all_gather(normed, "row", axis=0, tiled=True)
    gate_part = jnp.dot(block_piece, gate_weight, preferred_element_type=jnp.float32)
    up_part = jnp.dot(block_piece, up_weight, preferred_element_type=jnp.float32)
    partials = jnp.concatenate([gate_part, up_part], axis=1)
    hidden_width = gate_weight.shape[1]
    summed = lax.psum_scatter(partials, "col", scatter_dimension=0, tiled=True)
    hidden = (jax.nn.silu(summed[:, :hidden_width]) * summed[:, hidden_width:]).astype(jnp.bfloat16)
    down_terms = jnp.dot(
        lax.all_gather(hidden, "col", axis=0, tiled=True),
        down_weight,
        preferred_element_type=jnp.float32,
    )
    mlp_part = lax.psum_scatter(down_terms, "row", scatter_dimension=0, tiled=True)
    return (stream + mlp_part).astype(jnp.bfloat16)


def solution(mesh):
    in_specs = (
        P("col", "row"),
        P(None, ("row", "col"), None),
        P(None, ("row", "col"), None),
        P(None, "col", None),
        P(None, "col", None),
        P(),
        P("row", "col"),
        P("row", "col"),
        P("col"),
        P("col", "row"),
        P("col", "row"),
        P("row", "col"),
    )
    out_specs = P("row", "col")
    return jax.shard_map(local, mesh=mesh, in_specs=in_specs, out_specs=out_specs, check_vma=False)
```

profile of v0, /device:TPU:0, one launch (start us, length us, event | category | flops | bytes accessed | tf_op | source)
XLA Modules:
  0.0 490.5 jit_solution(6159983206683551800)
XLA Ops:
  6.6 1.5 gather_fusion
  8.1 0.1 fusion.48
  8.2 0.1 fusion.27
  8.4 0.7 gather_fusion.2
  9.1 2.3 gather_fusion.1
  11.5 2.1 maximum_select_fusion
  13.6 7.3 %all-to-all-start = ((bf16[32,128,256]{2,1,0:T(8,128)(2,1)}), bf16[32,128,256]{2,1,0:T(8,128)(2,1)S(1)}, u32[]{:S(2)}, u32[]{:S(2)}) async-start(bf16[32,128,256]{2,1,0:T(8,128)(2,1)} %maximum_select_fusion), calls=%async_computation | async-start | bytes 4194304 | tf_op jit(solution)/shard_map/all_to_all | solution.py:52
  20.9 0.0 all-gather.6.cloned.1.call-start
  21.0 0.1 reshape.272
  21.1 0.8 constant_dynamic-slice_fusion
  21.9 18.2 %all-gather.1 = bf16[1,512,128]{2,1,0:T(8,128)(2,1)S(1)} all-gather(bf16[1,128,128]{2,1,0:T(8,128)(2,1)S(1)} %constant_dynamic-slice_fusion), channel_id=3, replica_groups=mesh['row'=8,'col'=4] {'col'}, dimensions={1}, use_global_device_ids=true | all-gather | bytes 163840 | tf_op jit(solution)/shard_map/all_gather | solution.py:67
  40.0 0.8 constant_dynamic-slice_fusion.1
  40.8 10.9 %all-gather = bf16[1,512,128]{2,1,0:T(8,128)(2,1)S(1)} all-gather(bf16[1,128,128]{2,1,0:T(8,128)(2,1)S(1)} %constant_dynamic-slice_fusion.1), channel_id=2, replica_groups=mesh['row'=8,'col'=4] {'col'}, dimensions={1}, use_global_device_ids=true | all-gather | bytes 163840 | tf_op jit(solution)/shard_map/all_gather | solution.py:66
  51.7 0.7 fusion.42
  52.4 1.8 fusion.5
  54.2 15.4 %all-to-all-done = bf16[32,128,256]{2,1,0:T(8,128)(2,1)S(1)} async-done(((bf16[32,128,256]{2,1,0:T(8,128)(2,1)}), bf16[32,128,256]{2,1,0:T(8,128)(2,1)S(1)}, u32[]{:S(2)}, u32[]{:S(2)}) %all-to-all-start) | async-done | bytes 2097184 | tf_op jit(solution)/shard_map/all_to_all | solution.py:52
  69.6 0.6 gather_fusion.3
  70.2 1.3 multiply_reduce_fusion
  71.5 1.4 fusion
  72.9 0.1 copy-done.4
  73.0 0.6 fusion.7
  73.7 1.5 fusion.9
  75.1 0.8 fusion.12
  75.9 0.8 reshape.273
  76.8 0.0 all-gather.6.cloned.1.call-update
  76.8 0.0 reduce-scatter.4.cloned.1.call-start
  76.8 26.4 %all-gather.6.cloned.1.call-done = bf16[512,1024]{1,0:T(8,128)(2,1)} async-done(((bf16[128,1024]{1,0:T(8,128)(2,1)}), bf16[512,1024]{1,0:T(8,128)(2,1)}) %all-gather.6.cloned.1.call-update) | async-done | bytes 1048592 | tf_op jit(solution)/shard_map/all_gather | solution.py:80
  103.2 6.8 %fusion.50 = f32[512,2048]{1,0:T(8,128)} fusion(bf16[512,1024]{1,0:T(8,128)(2,1)} %all-gather.6.cloned.1.call-done, bf16[1024,2048]{1,0:T(8,128)(2,1)} %param.18), kind=kOutput, calls=%fused_computation.98 | convolution fusion | flops 2147483648 | bytes 9437184 | tf_op jit(solution)/shard_map/dot_general | solution.py:82
  110.0 0.0 reduce-scatter.4.cloned.1.call-update
  110.0 0.0 all-gather.8.cloned.1.call-start
  110.1 0.6 copy-done.6
  110.7 49.4 %reduce-scatter.4.cloned.1.call-done = f32[64,2048]{1,0:T(8,128)} async-done(((f32[512,2048]{1,0:T(8,128)}), f32[64,2048]{1,0:T(8,128)}) %reduce-scatter.4.cloned.1.call-update) | async-done | bytes 524304 | tf_op jit(solution)/shard_map/reduce_scatter | solution.py:81
  160.1 1.2 multiply_reduce_fusion.1
  161.3 9.8 %psum.7 = f32[64]{0:T(128)S(1)} all-reduce(f32[64]{0:T(128)S(1)} %multiply_reduce_fusion.1), channel_id=1, replica_groups=mesh['row'=8,'col'=4] {'col'}, use_global_device_ids=true, to_apply=%region_8.9 | all-reduce | flops 64 | bytes 512 | tf_op jit(solution)/shard_map/psum | solution.py:88
  171.2 1.9 multiply_convert_fusion
  173.1 0.2 reduce-scatter.6.cloned.1.call-start
  173.3 25.7 %all-gather.8.cloned.1.call-done = bf16[512,2048]{1,0:T(8,128)(2,1)} async-done(((bf16[64,2048]{1,0:T(8,128)(2,1)}), bf16[512,2048]{1,0:T(8,128)(2,1)}) %all-gather.8.cloned.1.call-update) | async-done | bytes 2097168 | tf_op jit(solution)/shard_map/all_gather | solution.py:92
  199.0 13.6 %fusion.52 = f32[512,3584]{1,0:T(8,128)S(1)} fusion(bf16[512,2048]{1,0:T(8,128)(2,1)} %all-gather.8.cloned.1.call-done, bf16[2048,3584]{1,0:T(8,128)(2,1)} %param.22), kind=kOutput, calls=%fused_computation.100 | convolution fusion | flops 7516192768 | bytes 24117248 | tf_op jit(solution)/shard_map/dot_general | solution.py:94
  212.6 11.0 %fusion.51 = f32[512,3584]{1,0:T(8,128)S(1)} fusion(bf16[512,2048]{1,0:T(8,128)(2,1)S(1)} %copy-done.7, bf16[2048,3584]{1,0:T(8,128)(2,1)} %param.21), kind=kOutput, calls=%fused_computation.99 | convolution fusion | flops 7516192768 | bytes 24117248 | tf_op jit(solution)/shard_map/dot_general | solution.py:93
  223.6 5.5 %pad_maximum_fusion = f32[512,7168]{1,0:T(8,128)} fusion(f32[512,3584]{1,0:T(8,128)S(1)} %fusion.52, f32[512,3584]{1,0:T(8,128)S(1)} %fusion.51), kind=kLoop, calls=%fused_computation.4 | loop fusion | flops 3670016 | bytes 29360128 | tf_op jit(solution)/shard_map/concatenate | solution.py:95
  229.2 0.0 all-gather.10.cloned.1.call-start
  229.2 137.2 %reduce-scatter.6.cloned.1.call-done = f32[128,7168]{1,0:T(8,128)} async-done(((f32[512,7168]{1,0:T(8,128)}), f32[128,7168]{1,0:T(8,128)}) %reduce-scatter.6.cloned.1.call-update) | async-done | bytes 3670032 | tf_op jit(solution)/shard_map/reduce_scatter | solution.py:97
  366.4 3.5 fusion.4
  369.9 0.0 reduce-scatter.8.cloned.1.call-start
  370.0 48.3 %all-gather.10.cloned.1.call-done = bf16[512,3584]{1,0:T(8,128)(2,1)} async-done(((bf16[128,3584]{1,0:T(8,128)(2,1)}), bf16[512,3584]{1,0:T(8,128)(2,1)}) %all-gather.10.cloned.1.call-update) | async-done | bytes 3670032 | tf_op jit(solution)/shard_map/all_gather | solution.py:100
  418.3 13.4 %fusion.53 = f32[512,2048]{1,0:T(8,128)} fusion(bf16[512,3584]{1,0:T(8,128)(2,1)} %all-gather.10.cloned.1.call-done, bf16[3584,2048]{1,0:T(8,128)(2,1)} %param.23), kind=kOutput, calls=%fused_computation.101 | convolution fusion | flops 7516192768 | bytes 22544384 | tf_op jit(solution)/shard_map/dot_general | solution.py:99
  431.7 50.1 %reduce-scatter.8.cloned.1.call-done = f32[64,2048]{1,0:T(8,128)} async-done(((f32[512,2048]{1,0:T(8,128)}), f32[64,2048]{1,0:T(8,128)}) %reduce-scatter.8.cloned.1.call-update) | async-done | bytes 524304 | tf_op jit(solution)/shard_map/reduce_scatter | solution.py:104
  481.8 1.8 add_convert_fusion
  (27 shorter events, 0.2 us)
Async XLA Ops:
  6.5 1.8 copy-start
  13.6 7.4 %copy-start.5 = (bf16[128,1024]{1,0:T(8,128)(2,1)S(1)}, bf16[128,1024]{1,0:T(8,128)(2,1)}, u32[]{:S(2)}) copy-start(bf16[128,1024]{1,0:T(8,128)(2,1)} %param.12) | copy-start | bytes 786436
  13.6 56.0 %all-to-all-start = ((bf16[32,128,256]{2,1,0:T(8,128)(2,1)}), bf16[32,128,256]{2,1,0:T(8,128)(2,1)S(1)}, u32[]{:S(2)}, u32[]{:S(2)}) async-start(bf16[32,128,256]{2,1,0:T(8,128)(2,1)} %maximum_select_fusion), calls=%async_computation | async-start | bytes 4194304 | tf_op jit(solution)/shard_map/all_to_all | solution.py:52
  20.9 82.4 %all-gather.6.cloned.1.call-start = ((), (), s32[]{:S(2)}) async-start(), calls=%async_computation.4 | async-start | bytes 1310720 | tf_op jit(solution)/shard_map/all_gather | solution.py:80
  71.5 1.6 copy-start.4
  76.8 83.3 %reduce-scatter.4.cloned.1.call-start = ((), (), s32[]{:S(2)}) async-start(), calls=%async_computation.5 | async-start | bytes 4718592 | tf_op jit(solution)/shard_map/reduce_scatter | solution.py:81
  110.0 0.7 copy-start.6
  110.0 50.1 %copy-start.3 = (bf16[64,2048]{1,0:T(8,128)(2,1)S(1)}, bf16[64,2048]{1,0:T(8,128)(2,1)}, u32[]{:S(2)}) copy-start(bf16[64,2048]{1,0:T(8,128)(2,1)} %param.19) | copy-start | bytes 786436
  110.0 89.0 %all-gather.8.cloned.1.call-start = ((), (), s32[]{:S(2)}) async-start(), calls=%async_computation.6 | async-start | bytes 2359296 | tf_op jit(solution)/shard_map/all_gather | solution.py:92
  173.1 193.4 %reduce-scatter.6.cloned.1.call-start = ((), (), s32[]{:S(2)}) async-start(), calls=%async_computation.7 | async-start | bytes 18350080 | tf_op jit(solution)/shard_map/reduce_scatter | solution.py:97
  199.0 13.6 %copy-start.7 = (bf16[512,2048]{1,0:T(8,128)(2,1)S(1)}, bf16[512,2048]{1,0:T(8,128)(2,1)}, u32[]{:S(2)}) copy-start(bf16[512,2048]{1,0:T(8,128)(2,1)} %all-gather.8.cloned.1.call-done) | copy-start | bytes 6291460
  229.2 189.1 %all-gather.10.cloned.1.call-start = ((), (), s32[]{:S(2)}) async-start(), calls=%async_computation.8 | async-start | bytes 4587520 | tf_op jit(solution)/shard_map/all_gather | solution.py:100
  369.9 111.9 %reduce-scatter.8.cloned.1.call-start = ((), (), s32[]{:S(2)}) async-start(), calls=%async_computation.9 | async-start | bytes 4718592 | tf_op jit(solution)/shard_map/reduce_scatter | solution.py:104
  431.7 51.9 %copy-start.1 = (bf16[8,1024,128]{2,1,0:T(8,128)(2,1)S(1)}, bf16[8,1024,128]{2,1,0:T(8,128)(2,1)}, u32[]{:S(2)}) copy-start(bf16[8,1024,128]{2,1,0:T(8,128)(2,1)} %param.14) | copy-start | bytes 6291460
  431.7 50.1 %copy-start.2 = (f32[64,2048]{1,0:T(8,128)S(1)}, f32[64,2048]{1,0:T(8,128)}, u32[]{:S(2)}) copy-start(f32[64,2048]{1,0:T(8,128)} %reduce-scatter.4.cloned.1.call-done) | copy-start | bytes 1572868
Sparse Core Ops, SparseCore 0:
  76.9 26.3 all-gather.5
  110.2 49.8 reduce-scatter.3
  173.2 25.8 all-gather.7
  229.3 137.1 reduce-scatter.5
  370.1 48.1 all-gather.9
  431.9 49.9 reduce-scatter.7
where the time goes:
time: 491 us; the launch traced here: 490 us
  waiting for transfers between devices  353 us (72%)
  matrix products  50 us (10%)
  blocking collectives  38.9 us (8%)
  other arithmetic  19 us (4%)
  between operations  13.7 us (3%)
  local copies, waits for them, and re-layouts  8.47 us (2%)
  starting transfers between devices  7.76 us (2%)
    reduce_scatter x1, waiting for transfers between devices, local(): summed = lax.psum_scatter(partials, 'col', scatter_dimension=0, tiled=True)  137 us
    reduce_scatter x1, waiting for transfers between devices, local(): lax.psum_scatter(down_terms, 'row', scatter_dimension=0, tiled=True)  50.1 us
    reduce_scatter x1, waiting for transfers between devices, local(): lax.psum_scatter(jnp.dot(all_attended, out_weight, preferred_element_type...  49.4 us
    all_gather x1, waiting for transfers between devices, local(): lax.all_gather(hidden, 'col', axis=0, tiled=True)  48.3 us
    all_gather x1, waiting for transfers between devices, local(): all_attended = lax.all_gather(attended, 'col', axis=0, tiled=True)  26.4 us
    all_gather x1, waiting for transfers between devices, local(): block_piece = lax.all_gather(normed, 'row', axis=0, tiled=True)  25.7 us
    all_gather x1, blocking collectives, local(): piece_values = lax.all_gather(own_values, 'col', axis=0, tiled=True)  18.2 us
    all_to_all x1, waiting for transfers between devices, local(): lax.all_to_all(outgoing, ('row', 'col'), split_axis=0, concat_axis=0, til...  15.4 us
  transfers between devices with their start and end apart: 7, of which 7 were waited for; matrix products, arithmetic and copies ran while one was open for 1% of the time, Pallas kernels for 0%

commit v1 on v0

--- a/solution.py
+++ b/solution.py
@@ -10,6 +10,7 @@
 HEAD_DIM = 128
 BLK = 128
 GROUP = 8
+CHUNKS = 2
 
 
 def local(
@@ -61,10 +62,11 @@
     run_sum = jnp.sum(far_exp, axis=1)
     run_acc = jnp.dot(far_exp.astype(jnp.bfloat16), far_values, preferred_element_type=jnp.float32)
     query_pos = col_index * BLK + jnp.arange(BLK * heads_here, dtype=jnp.int32) // heads_here
-    own_keys = lax.dynamic_index_in_dim(stretch_keys, my_group, 0, keepdims=False)
-    own_values = lax.dynamic_index_in_dim(stretch_values, my_group, 0, keepdims=False)
-    piece_keys = lax.all_gather(own_keys, "col", axis=0, tiled=True)
-    piece_values = lax.all_gather(own_values, "col", axis=0, tiled=True)
+    own = jnp.concatenate([stretch_keys, stretch_values], axis=2)
+    own = lax.dynamic_index_in_dim(own, my_group, 0, keepdims=False)
+    piece = lax.all_gather(own, "col", axis=0, tiled=True)
+    piece_keys = piece[:, :HEAD_DIM]
+    piece_values = piece[:, HEAD_DIM:]
     scores = jnp.dot(query_rows, piece_keys.T, preferred_element_type=jnp.float32) * scaling
     key_pos = jnp.arange(piece_keys.shape[0], dtype=jnp.int32)
     allowed = key_pos[None, :] <= query_pos[:, None]
@@ -79,30 +81,40 @@
     attended = (new_acc / new_sum[:, None]).astype(jnp.bfloat16).reshape(BLK, heads_here * HEAD_DIM)
     all_attended = lax.all_gather(attended, "col", axis=0, tiled=True)
     projected = lax.psum_scatter(
-        jnp.dot(all_attended, out_weight, preferred_element_type=jnp.float32),
+        jnp.dot(all_attended, out_weight, preferred_element_type=jnp.float32).astype(jnp.bfloat16),
         "row",
         scatter_dimension=0,
         tiled=True,
     )
-    stream = residual.astype(jnp.float32) + projected
-    squares = lax.psum(jnp.sum(stream * stream, axis=1), "col")
-    normed = (
-        stream * lax.rsqrt(squares / D + 1e-05)[:, None] * norm_gain.astype(jnp.float32)
-    ).astype(jnp.bfloat16)
-    block_piece = lax.all_gather(normed, "row", axis=0, tiled=True)
-    gate_part = jnp.dot(block_piece, gate_weight, preferred_element_type=jnp.float32)
-    up_part = jnp.dot(block_piece, up_weight, preferred_element_type=jnp.float32)
-    partials = jnp.concatenate([gate_part, up_part], axis=1)
+    stream = residual.astype(jnp.float32) + projected.astype(jnp.float32)
+    scaled = (stream * norm_gain.astype(jnp.float32)).astype(jnp.bfloat16)
+    block_piece = lax.all_gather(scaled, "row", axis=0, tiled=True)
+    own_squares = jnp.sum(stream * stream, axis=1)
+    all_squares = lax.all_gather(own_squares, ("row", "col"), axis=0)
+    squares = jnp.sum(all_squares.reshape(row_count, col_count, -1), axis=1).reshape(-1)
+    squares = lax.dynamic_slice_in_dim(squares, col_index * BLK, BLK)
+    factor = lax.rsqrt(squares / D + 1e-05)[:, None]
     hidden_width = gate_weight.shape[1]
-    summed = lax.psum_scatter(partials, "col", scatter_dimension=0, tiled=True)
-    hidden = (jax.nn.silu(summed[:, :hidden_width]) * summed[:, hidden_width:]).astype(jnp.bfloat16)
-    down_terms = jnp.dot(
-        lax.all_gather(hidden, "col", axis=0, tiled=True),
-        down_weight,
-        preferred_element_type=jnp.float32,
+    width = hidden_width // CHUNKS
+    down_terms = jnp.zeros((block_piece.shape[0], down_weight.shape[1]), jnp.float32)
+    for chunk in range(CHUNKS):
+        part = slice(chunk * width, (chunk + 1) * width)
+        gate_part = jnp.dot(block_piece, gate_weight[:, part], preferred_element_type=jnp.float32)
+        up_part = jnp.dot(block_piece, up_weight[:, part], preferred_element_type=jnp.float32)
+        partials = jnp.concatenate(
+            [gate_part.astype(jnp.bfloat16), up_part.astype(jnp.bfloat16)], axis=1
+        )
+        summed = lax.psum_scatter(partials, "col", scatter_dimension=0, tiled=True)
+        summed = summed.astype(jnp.float32) * factor
+        hidden = (jax.nn.silu(summed[:, :width]) * summed[:, width:]).astype(jnp.bfloat16)
+        gathered = lax.all_gather(hidden, "col", axis=0, tiled=True)
+        down_terms = down_terms + jnp.dot(
+            gathered, down_weight[part], preferred_element_type=jnp.float32
+        )
+    mlp_part = lax.psum_scatter(
+        down_terms.astype(jnp.bfloat16), "row", scatter_dimension=0, tiled=True
     )
-    mlp_part = lax.psum_scatter(down_terms, "row", scatter_dimension=0, tiled=True)
-    return (stream + mlp_part).astype(jnp.bfloat16)
+    return (stream + mlp_part.astype(jnp.float32)).astype(jnp.bfloat16)
 
 
 def solution(mesh):

time: 491 us -> 419 us (0.85)
  waiting for transfers between devices: 353 us -> 249 us
  blocking collectives: 38.9 us -> 61.7 us
  matrix products: 50 us -> 61 us
    reduce_scatter x1 -> x2, waiting for transfers between devices: 137 us -> 41.1 us  [local(): summed = lax.psum_scatter(partials, 'col', scatter_dimension=0, tiled=True)]
    unnamed x0 -> x1, blocking collectives: none -> 40.5 us
    reduce_scatter x1, waiting for transfers between devices: 49.4 us -> 35.5 us  [local(): lax.psum_scatter(jnp.dot(all_attended, out_weight, preferred_element_type...]
    reduce_scatter x1, waiting for transfers between devices: 50.1 us -> 36.2 us  [local(): lax.psum_scatter(down_terms.astype(jnp.bfloat16), 'row', scatter_dimensio...]
    dot_general x3 -> x6, matrix products: 38 us -> 49.5 us  [the longest x2 19.8 us: local(): jnp.dot(gathered, down_weight[part], preferred_element_type=jnp.float32)]
    all_gather x2 -> x3, waiting for transfers between devices: 74 us -> 84.8 us  [the longest x2 57 us: local(): gathered = lax.all_gather(hidden, 'col', axis=0, tiled=True)]
    psum x1 -> x0, blocking collectives: 9.85 us -> none  [local(): squares = lax.psum(jnp.sum(stream * stream, axis=1), 'col')]
    all_to_all x1, waiting for transfers between devices: 15.4 us -> 24.8 us  [local(): lax.all_to_all(outgoing, ('row', 'col'), split_axis=0, concat_axis=0, til...]
  transfers between devices with their start and end apart: 7 -> 9, of which waited for: 7 -> 8; matrix products, arithmetic and copies ran while one was open for 1% -> 7% of each run, Pallas kernels for 0% -> 0%
where the time goes in v1:
time: 419 us; the launch traced here: 418 us
  waiting for transfers between devices  249 us (59%)
  blocking collectives  61.7 us (15%)
  matrix products  61 us (15%)
  other arithmetic  16.9 us (4%)
  between operations  13.8 us (3%)
  starting transfers between devices  8.32 us (2%)
  local copies, waits for them, and re-layouts  7.39 us (2%)
    all_gather x2, waiting for transfers between devices, local(): gathered = lax.all_gather(hidden, 'col', axis=0, tiled=True)  57 us
    reduce_scatter x2, waiting for transfers between devices, local(): summed = lax.psum_scatter(partials, 'col', scatter_dimension=0, tiled=True)  41.1 us
    unnamed x1, blocking collectives  40.5 us
    reduce_scatter x1, waiting for transfers between devices, local(): lax.psum_scatter(down_terms.astype(jnp.bfloat16), 'row', scatter_dimensio...  36.2 us
    reduce_scatter x1, waiting for transfers between devices, local(): lax.psum_scatter(jnp.dot(all_attended, out_weight, preferred_element_type...  35.5 us
    all_gather x1, waiting for transfers between devices, local(): block_piece = lax.all_gather(scaled, 'row', axis=0, tiled=True)  27.7 us
    all_gather x1, waiting for transfers between devices, local(): all_attended = lax.all_gather(attended, 'col', axis=0, tiled=True)  26.4 us
    all_to_all x1, waiting for transfers between devices, local(): lax.all_to_all(outgoing, ('row', 'col'), split_axis=0, concat_axis=0, til...  24.8 us
  transfers between devices with their start and end apart: 9, of which 8 were waited for; matrix products, arithmetic and copies ran while one was open for 7% of the time, Pallas kernels for 0%

profile of v1, /device:TPU:0, one launch (start us, length us, event | category | flops | bytes accessed | tf_op | source)
XLA Modules:
  0.0 418.0 jit_solution(18146797939492085028)
XLA Ops:
  6.6 1.5 gather_fusion
  8.1 0.1 fusion.76
  8.2 0.1 fusion.55
  8.4 0.7 gather_fusion.1
  9.1 2.3 gather_fusion.2
  11.5 2.1 maximum_select_fusion
  13.6 7.3 %all-to-all-start = ((bf16[32,128,256]{2,1,0:T(8,128)(2,1)}), bf16[32,128,256]{2,1,0:T(8,128)(2,1)S(1)}, u32[]{:S(2)}, u32[]{:S(2)}) async-start(bf16[32,128,256]{2,1,0:T(8,128)(2,1)} %maximum_select_fusion), calls=%async_computation | async-start | bytes 4194304 | tf_op jit(solution)/shard_map/all_to_all | solution.py:53
  21.0 0.1 reshape.278
  21.1 21.1 %all-gather = bf16[1,512,256]{2,1,0:T(8,128)(2,1)S(1)} all-gather(bf16[1,128,256]{2,1,0:T(8,128)(2,1)S(1)} %fusion.52), channel_id=2, replica_groups=mesh['row'=8,'col'=4] {'col'}, dimensions={1}, use_global_device_ids=true | all-gather | bytes 327680 | tf_op jit(solution)/shard_map/all_gather | solution.py:67
  42.3 0.7 fusion.70
  43.0 1.8 fusion.30
  44.8 24.8 %all-to-all-done = bf16[32,128,256]{2,1,0:T(8,128)(2,1)S(1)} async-done(((bf16[32,128,256]{2,1,0:T(8,128)(2,1)}), bf16[32,128,256]{2,1,0:T(8,128)(2,1)S(1)}, u32[]{:S(2)}, u32[]{:S(2)}) %all-to-all-start) | async-done | bytes 2097184 | tf_op jit(solution)/shard_map/all_to_all | solution.py:53
  69.6 0.6 gather_fusion.3
  70.2 1.3 multiply_reduce_fusion
  71.5 1.4 fusion.12
  72.9 0.1 copy-done.2
  73.0 0.6 fusion.32
  73.7 1.5 fusion.34
  75.2 0.8 fusion.37
  76.0 0.8 reshape.279
  76.8 26.4 %all-gather.7.cloned.1.call-done = bf16[512,1024]{1,0:T(8,128)(2,1)} async-done(((bf16[128,1024]{1,0:T(8,128)(2,1)}), bf16[512,1024]{1,0:T(8,128)(2,1)}) %all-gather.7.cloned.1.call-update) | async-done | bytes 1048592 | tf_op jit(solution)/shard_map/all_gather | solution.py:82
  103.3 6.2 %convolution_convert_fusion = bf16[512,2048]{1,0:T(8,128)(2,1)} fusion(bf16[512,1024]{1,0:T(8,128)(2,1)} %all-gather.7.cloned.1.call-done, bf16[1024,2048]{1,0:T(8,128)(2,1)} %param.18), kind=kOutput, calls=%fused_computation.24 | convolution fusion | flops 2148532224 | bytes 7340032 | tf_op jit(solution)/shard_map/dot_general | solution.py:84
  109.5 0.6 copy-done.10
  110.2 35.5 %reduce-scatter.5.cloned.1.call-done = bf16[64,2048]{1,0:T(8,128)(2,1)} async-done(((bf16[512,2048]{1,0:T(8,128)(2,1)}), bf16[64,2048]{1,0:T(8,128)(2,1)}) %reduce-scatter.5.cloned.1.call-update) | async-done | bytes 262160 | tf_op jit(solution)/shard_map/reduce_scatter | solution.py:83
  145.7 1.9 multiply_reduce_fusion.1
  147.6 0.2 reduce-scatter.9.cloned.1.call-start
  147.8 27.7 %all-gather.9.cloned.1.call-done = bf16[512,2048]{1,0:T(8,128)(2,1)} async-done(((bf16[64,2048]{1,0:T(8,128)(2,1)}), bf16[512,2048]{1,0:T(8,128)(2,1)}) %all-gather.9.cloned.1.call-update) | async-done | bytes 2097168 | tf_op jit(solution)/shard_map/all_gather | solution.py:91
  175.5 7.8 %fusion.24 = bf16[512,1792]{1,0:T(8,128)(2,1)S(1)} fusion(bf16[512,2048]{1,0:T(8,128)(2,1)} %all-gather.9.cloned.1.call-done, bf16[2048,3584]{1,0:T(8,128)(2,1)} %param.21), kind=kOutput, calls=%fused_computation.27 | convolution fusion | flops 3759013888 | bytes 11272192 | tf_op jit(solution)/shard_map/dot_general | solution.py:102
  183.4 7.1 %fusion.27 = bf16[512,1792]{1,0:T(8,128)(2,1)S(1)} fusion(bf16[512,2048]{1,0:T(8,128)(2,1)S(1)} %copy-done.11, bf16[2048,3584]{1,0:T(8,128)(2,1)} %param.22), kind=kOutput, calls=%fused_computation.28 | convolution fusion | flops 3759013888 | bytes 11272192 | tf_op jit(solution)/shard_map/dot_general | solution.py:103
  190.4 2.1 pad_maximum_fusion.1
  192.5 0.3 reduce-scatter.7.cloned.1.call-start
  192.8 7.8 %fusion.18 = bf16[512,1792]{1,0:T(8,128)(2,1)S(1)} fusion(bf16[512,2048]{1,0:T(8,128)(2,1)} %all-gather.9.cloned.1.call-done, bf16[2048,3584]{1,0:T(8,128)(2,1)} %param.21), kind=kOutput, calls=%fused_computation.25 | convolution fusion | flops 3759013888 | bytes 11272192 | tf_op jit(solution)/shard_map/dot_general | solution.py:102
  200.6 7.1 %fusion.21 = bf16[512,1792]{1,0:T(8,128)(2,1)S(1)} fusion(bf16[512,2048]{1,0:T(8,128)(2,1)S(1)} %copy-done.12, bf16[2048,3584]{1,0:T(8,128)(2,1)} %param.22), kind=kOutput, calls=%fused_computation.26 | convolution fusion | flops 3759013888 | bytes 11272192 | tf_op jit(solution)/shard_map/dot_general | solution.py:103
  207.7 2.1 pad_maximum_fusion
  209.9 0.3 dynamic-update-slice
  210.2 40.5 %all-reduce = f32[2048]{0:T(1024)S(1)} all-reduce(f32[2048]{0:T(1024)S(1)} %dynamic-update-slice), channel_id=3, replica_groups=mesh['row'=8,'col'=4] {'row','col'}, use_global_device_ids=true, to_apply=%add | all-reduce | flops 2048 | bytes 16384
  250.9 0.1 add_rsqrt_fusion
  251.0 41.1 %reduce-scatter.7.cloned.1.call-done = bf16[128,3584]{1,0:T(8,128)(2,1)} async-done(((bf16[512,3584]{1,0:T(8,128)(2,1)}), bf16[128,3584]{1,0:T(8,128)(2,1)}) %reduce-scatter.7.cloned.1.call-update) | async-done | bytes 917520 | tf_op jit(solution)/shard_map/reduce_scatter | solution.py:107
  292.1 1.8 convert_multiply_fusion.1
  293.8 1.0 fusion.44
  294.9 1.1 fusion.45
  296.0 0.3 reduce-scatter.11.cloned.1.call-start
  296.4 31.7 %all-gather.13.cloned.1.call-done = bf16[512,1792]{1,0:T(8,128)(2,1)} async-done(((bf16[128,1792]{1,0:T(8,128)(2,1)}), bf16[512,1792]{1,0:T(8,128)(2,1)}) %all-gather.13.cloned.1.call-update) | async-done | bytes 1835024 | tf_op jit(solution)/shard_map/all_gather | solution.py:110
  328.1 9.5 %fusion = f32[512,2048]{1,0:T(8,128)} fusion(bf16[512,1792]{1,0:T(8,128)(2,1)} %all-gather.13.cloned.1.call-done, bf16[3584,2048]{1,0:T(8,128)(2,1)} %param.23), kind=kOutput, calls=%fused_computation.6 | convolution fusion | flops 3758096384 | bytes 13369344 | tf_op jit(solution)/shard_map/dot_general | solution.py:111
  337.6 25.3 %all-gather.11.cloned.1.call-done = bf16[512,1792]{1,0:T(8,128)(2,1)} async-done(((bf16[128,1792]{1,0:T(8,128)(2,1)}), bf16[512,1792]{1,0:T(8,128)(2,1)}) %all-gather.11.cloned.1.call-update) | async-done | bytes 1835024 | tf_op jit(solution)/shard_map/all_gather | solution.py:110
  363.0 10.2 %add_convert_fusion = bf16[512,2048]{1,0:T(8,128)(2,1)} fusion(f32[512,2048]{1,0:T(8,128)} %fusion, bf16[512,1792]{1,0:T(8,128)(2,1)} %all-gather.11.cloned.1.call-done, bf16[3584,2048]{1,0:T(8,128)(2,1)} %param.23), kind=kOutput, calls=%fused_computation.20 | convolution fusion | flops 3760193536 | bytes 15466496 | tf_op jit(solution)/shard_map/dot_general | solution.py:111
  373.2 36.2 %reduce-scatter.11.cloned.1.call-done = bf16[64,2048]{1,0:T(8,128)(2,1)} async-done(((bf16[512,2048]{1,0:T(8,128)(2,1)}), bf16[64,2048]{1,0:T(8,128)(2,1)}) %reduce-scatter.11.cloned.1.call-update) | async-done | bytes 262160 | tf_op jit(solution)/shard_map/reduce_scatter | solution.py:114
  409.4 1.7 add_convert_fusion.1
  (51 shorter events, 0.7 us)
Async XLA Ops:
  6.5 1.8 copy-start
  13.6 7.4 %copy-start.7 = (bf16[128,1024]{1,0:T(8,128)(2,1)S(1)}, bf16[128,1024]{1,0:T(8,128)(2,1)}, u32[]{:S(2)}) copy-start(bf16[128,1024]{1,0:T(8,128)(2,1)} %param.12) | copy-start | bytes 786436
  13.6 7.5 %copy-start.8 = (bf16[8,128,128]{2,1,0:T(8,128)(2,1)S(1)}, bf16[8,128,128]{2,1,0:T(8,128)(2,1)}, u32[]{:S(2)}) copy-start(bf16[8,128,128]{2,1,0:T(8,128)(2,1)} %param.15) | copy-start | bytes 786436
  13.6 7.6 %copy-start.9 = (bf16[8,128,128]{2,1,0:T(8,128)(2,1)S(1)}, bf16[8,128,128]{2,1,0:T(8,128)(2,1)}, u32[]{:S(2)}) copy-start(bf16[8,128,128]{2,1,0:T(8,128)(2,1)} %param.16) | copy-start | bytes 786436
  13.6 56.0 %all-to-all-start = ((bf16[32,128,256]{2,1,0:T(8,128)(2,1)}), bf16[32,128,256]{2,1,0:T(8,128)(2,1)S(1)}, u32[]{:S(2)}, u32[]{:S(2)}) async-start(bf16[32,128,256]{2,1,0:T(8,128)(2,1)} %maximum_select_fusion), calls=%async_computation | async-start | bytes 4194304 | tf_op jit(solution)/shard_map/all_to_all | solution.py:53
  20.9 82.4 %all-gather.7.cloned.1.call-start = ((), (), s32[]{:S(2)}) async-start(), calls=%async_computation.5 | async-start | bytes 1310720 | tf_op jit(solution)/shard_map/all_gather | solution.py:82
  42.3 0.7 copy-start.5
  71.4 1.6 copy-start.2
  73.6 1.5 copy-start.6
  76.8 68.9 %reduce-scatter.5.cloned.1.call-start = ((), (), s32[]{:S(2)}) async-start(), calls=%async_computation.6 | async-start | bytes 2359296 | tf_op jit(solution)/shard_map/reduce_scatter | solution.py:83
  109.5 0.7 copy-start.10
  109.5 36.2 %copy-start.3 = (bf16[64,2048]{1,0:T(8,128)(2,1)S(1)}, bf16[64,2048]{1,0:T(8,128)(2,1)}, u32[]{:S(2)}) copy-start(bf16[64,2048]{1,0:T(8,128)(2,1)} %param.19) | copy-start | bytes 786436
  109.5 66.0 %all-gather.9.cloned.1.call-start = ((), (), s32[]{:S(2)}) async-start(), calls=%async_computation.7 | async-start | bytes 2359296 | tf_op jit(solution)/shard_map/all_gather | solution.py:91
  147.6 103.4 %reduce-scatter.9.cloned.1.call-start = ((), (), s32[]{:S(2)}) async-start(), calls=%async_computation.10 | async-start | bytes 4587520 | tf_op jit(solution)/shard_map/reduce_scatter | solution.py:107
  175.5 7.8 %copy-start.11 = (bf16[512,2048]{1,0:T(8,128)(2,1)S(1)}, bf16[512,2048]{1,0:T(8,128)(2,1)}, u32[]{:S(2)}) copy-start(bf16[512,2048]{1,0:T(8,128)(2,1)} %all-gather.9.cloned.1.call-done) | copy-start | bytes 6291460
  192.5 99.5 %reduce-scatter.7.cloned.1.call-start = ((), (), s32[]{:S(2)}) async-start(), calls=%async_computation.8 | async-start | bytes 4587520 | tf_op jit(solution)/shard_map/reduce_scatter | solution.py:107
  192.8 7.8 %copy-start.12 = (bf16[512,2048]{1,0:T(8,128)(2,1)S(1)}, bf16[512,2048]{1,0:T(8,128)(2,1)}, u32[]{:S(2)}) copy-start(bf16[512,2048]{1,0:T(8,128)(2,1)} %all-gather.9.cloned.1.call-done) | copy-start | bytes 6291460
  209.8 118.3 %all-gather.13.cloned.1.call-start = ((), (), s32[]{:S(2)}) async-start(), calls=%async_computation.11 | async-start | bytes 2293760 | tf_op jit(solution)/shard_map/all_gather | solution.py:110
  294.9 68.1 %all-gather.11.cloned.1.call-start = ((), (), s32[]{:S(2)}) async-start(), calls=%async_computation.9 | async-start | bytes 2293760 | tf_op jit(solution)/shard_map/all_gather | solution.py:110
  296.0 113.4 %reduce-scatter.11.cloned.1.call-start = ((), (), s32[]{:S(2)}) async-start(), calls=%async_computation.12 | async-start | bytes 2359296 | tf_op jit(solution)/shard_map/reduce_scatter | solution.py:114
  362.9 48.2 %copy-start.1 = (bf16[8,1024,128]{2,1,0:T(8,128)(2,1)S(1)}, bf16[8,1024,128]{2,1,0:T(8,128)(2,1)}, u32[]{:S(2)}) copy-start(bf16[8,1024,128]{2,1,0:T(8,128)(2,1)} %param.13) | copy-start | bytes 6291460
  373.2 36.3 %copy-start.4 = (bf16[64,2048]{1,0:T(8,128)(2,1)S(1)}, bf16[64,2048]{1,0:T(8,128)(2,1)}, u32[]{:S(2)}) copy-start(bf16[64,2048]{1,0:T(8,128)(2,1)} %reduce-scatter.5.cloned.1.call-done) | copy-start | bytes 786436
Sparse Core Ops, SparseCore 0:
  76.9 26.3 all-gather.6
  109.6 36.0 reduce-scatter.4
  147.7 27.7 all-gather.8
  192.6 48.2 reduce-scatter.8
  243.8 48.2 reduce-scatter.6
  295.0 33.0 all-gather.12
  329.9 32.9 all-gather.10
  373.3 36.0 reduce-scatter.10

commit v2 on v1

--- a/solution.py
+++ b/solution.py
@@ -1,8 +1,11 @@
+import functools
 import math
 
 import jax
 import jax.numpy as jnp
 from jax import lax
+from jax.experimental import pallas as pl
+from jax.experimental.pallas import tpu as pltpu
 from jax.sharding import PartitionSpec as P
 
 D = 8192
@@ -10,7 +13,221 @@
 HEAD_DIM = 128
 BLK = 128
 GROUP = 8
-CHUNKS = 2
+WIDTH = 256
+SLOTS = 3
+MESH = pl.DeviceIdType.MESH
+
+
+def feed_forward_kernel(
+    peers,
+    chunks,
+    pieces_ref,
+    squares_ref,
+    gate_ref,
+    up_ref,
+    down_ref,
+    out_ref,
+    gate_buf,
+    up_buf,
+    down_buf,
+    part_buf,
+    sums_buf,
+    hidden_buf,
+    square_buf,
+    factor_buf,
+    total,
+    gate_sem,
+    up_sem,
+    down_sem,
+    sums_send,
+    sums_recv,
+    hidden_send,
+    hidden_recv,
+    square_send,
+    square_recv,
+):
+    me = lax.axis_index("col")
+    depth = gate_ref.shape[0]
+
+    def target(k):
+        return lax.rem(me + k, peers)
+
+    def sums_copy(j, k):
+        slot = lax.rem(j, SLOTS)
+        return pltpu.make_async_remote_copy(
+            src_ref=part_buf.at[slot, target(k)],
+            dst_ref=sums_buf.at[slot, k - 1],
+            send_sem=sums_send.at[slot, k - 1],
+            recv_sem=sums_recv.at[slot, k - 1],
+            device_id={"col": target(k)},
+            device_id_type=MESH,
+        )
+
+    def hidden_copy(j, k):
+        slot = lax.rem(j, SLOTS)
+        return pltpu.make_async_remote_copy(
+            src_ref=hidden_buf.at[slot, 0],
+            dst_ref=hidden_buf.at[slot, k],
+            send_sem=hidden_send.at[slot, k - 1],
+            recv_sem=hidden_recv.at[slot, k - 1],
+            device_id={"col": target(k)},
+            device_id_type=MESH,
+        )
+
+    def square_copy(k):
+        return pltpu.make_async_remote_copy(
+            src_ref=squares_ref.at[target(k)],
+            dst_ref=square_buf.at[k - 1],
+            send_sem=square_send.at[k - 1],
+            recv_sem=square_recv.at[k - 1],
+            device_id={"col": target(k)},
+            device_id_type=MESH,
+        )
+
+    def columns(j):
+        return pl.ds(pl.multiple_of(j * WIDTH, WIDTH), WIDTH)
+
+    def gate_copy(j):
+        slot = lax.rem(j, 2)
+        return pltpu.make_async_copy(
+            gate_ref.at[:, columns(j)], gate_buf.at[slot], gate_sem.at[slot]
+        )
+
+    def up_copy(j):
+        slot = lax.rem(j, 2)
+        return pltpu.make_async_copy(up_ref.at[:, columns(j)], up_buf.at[slot], up_sem.at[slot])
+
+    def down_copy(j):
+        slot = lax.rem(j, 2)
+        return pltpu.make_async_copy(
+            down_ref.at[columns(j), :], down_buf.at[slot], down_sem.at[slot]
+        )
+
+    gate_copy(0).start()
+    up_copy(0).start()
+    down_copy(0).start()
+    barrier = pltpu.get_barrier_semaphore()
+    for k in range(1, peers):
+        pl.semaphore_signal(barrier, inc=1, device_id={"col": target(k)}, device_id_type=MESH)
+    pl.semaphore_wait(barrier, peers - 1)
+    for k in range(1, peers):
+        square_copy(k).start()
+    total[...] = jnp.zeros_like(total)
+
+    def step(i, carry):
+        @pl.when(i < chunks)
+        def _():
+            @pl.when(i + 1 < chunks)
+            def _():
+                gate_copy(i + 1).start()
+                up_copy(i + 1).start()
+
+            slot = lax.rem(i, SLOTS)
+            for position, (copy, buf) in enumerate(((gate_copy, gate_buf), (up_copy, up_buf))):
+                copy(i).wait()
+                product = jnp.dot(
+                    pieces_ref[:, :depth],
+                    buf[lax.rem(i, 2)],
+                    preferred_element_type=jnp.float32,
+                ).astype(jnp.bfloat16)
+                part_buf[slot, :, :, position * WIDTH : (position + 1) * WIDTH] = product.reshape(
+                    peers, BLK, WIDTH
+                )
+            for k in range(1, peers):
+                sums_copy(i, k).start()
+
+        @pl.when(i == 1)
+        def _():
+            squares = squares_ref[me]
+            for k in range(1, peers):
+                square_copy(k).wait()
+                squares = squares + square_buf[k - 1]
+            factor_buf[...] = lax.rsqrt(squares / D + 1e-05)
+
+        @pl.when((i >= 1) & (i < chunks + 1))
+        def _():
+            j = i - 1
+            slot = lax.rem(j, SLOTS)
+            summed = part_buf[slot, me].astype(jnp.float32)
+            for k in range(1, peers):
+                sums_copy(j, k).wait()
+                summed = summed + sums_buf[slot, k - 1].astype(jnp.float32)
+            summed = summed * factor_buf[:, :1]
+            gate = summed[:, :WIDTH]
+            hidden_buf[slot, 0] = (
+                gate / (1.0 + jnp.exp(-gate)) * summed[:, WIDTH:]
+            ).astype(jnp.bfloat16)
+            for k in range(1, peers):
+                hidden_copy(j, k).start()
+
+        @pl.when(i >= 2)
+        def _():
+            j = i - 2
+            slot = lax.rem(j, SLOTS)
+
+            @pl.when(j + 1 < chunks)
+            def _():
+                down_copy(j + 1).start()
+
+            down_copy(j).wait()
+            for k in range(1, peers):
+                hidden_copy(j, k).wait()
+            gathered = hidden_buf[slot].reshape(peers * BLK, WIDTH)
+            out_width = total.shape[1]
+            tile = min(512, out_width)
+            for start in range(0, out_width, tile):
+                total[:, start : start + tile] += jnp.dot(
+                    gathered,
+                    down_buf[lax.rem(j, 2), :, start : start + tile],
+                    preferred_element_type=jnp.float32,
+                )
+
+        return carry
+
+    lax.fori_loop(0, chunks + 2, step, 0)
+    for k in range(peers):
+        owner = lax.rem(me + peers - k, peers)
+        out_ref[owner] = total[k * BLK : (k + 1) * BLK, :].astype(jnp.bfloat16)
+
+
+def feed_forward(pieces, squares, gate_weight, up_weight, down_weight):
+    peers = lax.axis_size("col")
+    depth, hidden_width = gate_weight.shape
+    out_width = down_weight.shape[1]
+    chunks = hidden_width // WIDTH
+    vmem = pl.BlockSpec(memory_space=pltpu.VMEM)
+    hbm = pl.BlockSpec(memory_space=pl.ANY)
+    pair = (SLOTS, peers - 1)
+    dma = pltpu.SemaphoreType.DMA
+    return pl.pallas_call(
+        functools.partial(feed_forward_kernel, peers, chunks),
+        out_shape=jax.ShapeDtypeStruct((peers, BLK, out_width), jnp.bfloat16),
+        in_specs=[vmem, vmem, hbm, hbm, hbm],
+        out_specs=vmem,
+        scratch_shapes=[
+            pltpu.VMEM((2, depth, WIDTH), jnp.bfloat16),
+            pltpu.VMEM((2, depth, WIDTH), jnp.bfloat16),
+            pltpu.VMEM((2, WIDTH, out_width), jnp.bfloat16),
+            pltpu.VMEM((SLOTS, peers, BLK, 2 * WIDTH), jnp.bfloat16),
+            pltpu.VMEM((SLOTS, peers - 1, BLK, 2 * WIDTH), jnp.bfloat16),
+            pltpu.VMEM((SLOTS, peers, BLK, WIDTH), jnp.bfloat16),
+            pltpu.VMEM((peers - 1, BLK, 128), jnp.float32),
+            pltpu.VMEM((BLK, 128), jnp.float32),
+            pltpu.VMEM((peers * BLK, out_width), jnp.float32),
+            dma((2,)),
+            dma((2,)),
+            dma((2,)),
+            dma(pair),
+            dma(pair),
+            dma(pair),
+            dma(pair),
+            dma((peers - 1,)),
+            dma((peers - 1,)),
+        ],
+        compiler_params=pltpu.CompilerParams(
+            collective_id=0, has_side_effects=True, vmem_limit_bytes=48 * 1024 * 1024
+        ),
+    )(pieces, squares, gate_weight, up_weight, down_weight)
 
 
 def local(
@@ -88,31 +305,20 @@
     )
     stream = residual.astype(jnp.float32) + projected.astype(jnp.float32)
     scaled = (stream * norm_gain.astype(jnp.float32)).astype(jnp.bfloat16)
-    block_piece = lax.all_gather(scaled, "row", axis=0, tiled=True)
-    own_squares = jnp.sum(stream * stream, axis=1)
-    all_squares = lax.all_gather(own_squares, ("row", "col"), axis=0)
-    squares = jnp.sum(all_squares.reshape(row_count, col_count, -1), axis=1).reshape(-1)
-    squares = lax.dynamic_slice_in_dim(squares, col_index * BLK, BLK)
-    factor = lax.rsqrt(squares / D + 1e-05)[:, None]
-    hidden_width = gate_weight.shape[1]
-    width = hidden_width // CHUNKS
-    down_terms = jnp.zeros((block_piece.shape[0], down_weight.shape[1]), jnp.float32)
-    for chunk in range(CHUNKS):
-        part = slice(chunk * width, (chunk + 1) * width)
-        gate_part = jnp.dot(block_piece, gate_weight[:, part], preferred_element_type=jnp.float32)
-        up_part = jnp.dot(block_piece, up_weight[:, part], preferred_element_type=jnp.float32)
-        partials = jnp.concatenate(
-            [gate_part.astype(jnp.bfloat16), up_part.astype(jnp.bfloat16)], axis=1
-        )
-        summed = lax.psum_scatter(partials, "col", scatter_dimension=0, tiled=True)
-        summed = summed.astype(jnp.float32) * factor
-        hidden = (jax.nn.silu(summed[:, :width]) * summed[:, width:]).astype(jnp.bfloat16)
-        gathered = lax.all_gather(hidden, "col", axis=0, tiled=True)
-        down_terms = down_terms + jnp.dot(
-            gathered, down_weight[part], preferred_element_type=jnp.float32
-        )
+    rest = jnp.sum(stream * stream, axis=1, keepdims=True)
+    terms = []
+    for _ in range(3):
+        term = lax.reduce_precision(rest, exponent_bits=8, mantissa_bits=7)
+        terms.append(term)
+        rest = rest - term
+    riders = jnp.concatenate(terms + [jnp.zeros((rest.shape[0], 125), jnp.float32)], axis=1)
+    outgoing_piece = jnp.concatenate([scaled, riders.astype(jnp.bfloat16)], axis=1)
+    pieces = lax.all_gather(outgoing_piece, "row", axis=0, tiled=True)
+    squares = jnp.sum(pieces[:, scaled.shape[1] :].astype(jnp.float32), axis=1, keepdims=True)
+    squares = jnp.broadcast_to(squares, (squares.shape[0], 128)).reshape(col_count, BLK, 128)
+    down_terms = feed_forward(pieces, squares, gate_weight, up_weight, down_weight)
     mlp_part = lax.psum_scatter(
-        down_terms.astype(jnp.bfloat16), "row", scatter_dimension=0, tiled=True
+        down_terms.reshape(-1, down_terms.shape[2]), "row", scatter_dimension=0, tiled=True
     )
     return (stream + mlp_part.astype(jnp.float32)).astype(jnp.bfloat16)
 

time: 419 us -> 352 us (0.84)
  Pallas kernels: 0 us -> 127 us
  waiting for transfers between devices: 249 us -> 151 us
  matrix products: 61 us -> 11.5 us
  blocking collectives: 61.7 us -> 21.1 us
  other arithmetic: 16.9 us -> 9.04 us
    pallas_call x0 -> x1, Pallas kernels: none -> 127 us  [feed_forward(): pl.pallas_call(functools.partial(feed_forward_kernel, peers, chunks), out...]
    all_gather x3 -> x1, waiting for transfers between devices: 84.8 us -> 28.8 us  [local(): pieces = lax.all_gather(outgoing_piece, 'row', axis=0, tiled=True)]
    dot_general x6 -> x0, matrix products: 49.5 us -> none  [the longest x2 19.8 us: local(): jnp.dot(gathered, down_weight[part], preferred_element_type=jnp.float32)]
    reduce_scatter x3 -> x1, waiting for transfers between devices: 77.3 us -> 35.4 us  [local(): lax.psum_scatter(down_terms.reshape(-1, down_terms.shape[2]), 'row', scat...]
    unnamed x1 -> x0, blocking collectives: 40.5 us -> none
  transfers between devices with their start and end apart: 9 -> 5, of which waited for: 8 -> 5; matrix products, arithmetic and copies ran while one was open for 7% -> 1% of each run, Pallas kernels for 0% -> 0%
where the time goes in v2:
time: 352 us; the launch traced here: 351 us
  waiting for transfers between devices  151 us (43%)
  Pallas kernels  127 us (36%)
  blocking collectives  21.1 us (6%)
  between operations  13.4 us (4%)
  matrix products  11.5 us (3%)
  local copies, waits for them, and re-layouts  11.1 us (3%)
  other arithmetic  9.04 us (3%)
  starting transfers between devices  7.67 us (2%)
    pallas_call x1, Pallas kernels, feed_forward(): pl.pallas_call(functools.partial(feed_forward_kernel, peers, chunks), out...  127 us
    reduce_scatter x1, waiting for transfers between devices, local(): lax.psum_scatter(jnp.dot(all_attended, out_weight, preferred_element_type...  35.5 us
    reduce_scatter x1, waiting for transfers between devices, local(): lax.psum_scatter(down_terms.reshape(-1, down_terms.shape[2]), 'row', scat...  35.4 us
    all_gather x1, waiting for transfers between devices, local(): pieces = lax.all_gather(outgoing_piece, 'row', axis=0, tiled=True)  28.8 us
    all_gather x1, waiting for transfers between devices, local(): all_attended = lax.all_gather(attended, 'col', axis=0, tiled=True)  26.4 us
    all_to_all x1, waiting for transfers between devices, local(): lax.all_to_all(outgoing, ('row', 'col'), split_axis=0, concat_axis=0, til...  24.8 us
    all_gather x1, blocking collectives, local(): piece = lax.all_gather(own, 'col', axis=0, tiled=True)  21.1 us
    all_to_all x1, starting transfers between devices, local(): lax.all_to_all(outgoing, ('row', 'col'), split_axis=0, concat_axis=0, til...  7.33 us
  transfers between devices with their start and end apart: 5, of which 5 were waited for; matrix products, arithmetic and copies ran while one was open for 1% of the time, Pallas kernels for 0%

profile of v2, /device:TPU:0, one launch (start us, length us, event | category | flops | bytes accessed | tf_op | source)
XLA Modules:
  0.0 351.3 jit_solution(12946907386172485441)
XLA Ops:
  6.5 0.0 copy-start
  6.6 1.5 gather_fusion
  8.1 0.1 fusion.51
  8.2 0.1 fusion.29
  8.4 0.7 gather_fusion.1
  9.1 2.3 gather_fusion.2
  11.5 2.0 maximum_select_fusion
  13.5 7.3 %all-to-all-start = ((bf16[32,128,256]{2,1,0:T(8,128)(2,1)}), bf16[32,128,256]{2,1,0:T(8,128)(2,1)S(1)}, u32[]{:S(2)}, u32[]{:S(2)}) async-start(bf16[32,128,256]{2,1,0:T(8,128)(2,1)} %maximum_select_fusion), calls=%async_computation | async-start | bytes 4194304 | tf_op jit(solution)/shard_map/all_to_all | solution.py:270
  20.9 0.0 all-gather.4.cloned.1.call-start
  20.9 0.1 reshape.313
  21.1 21.1 %all-gather = bf16[1,512,256]{2,1,0:T(8,128)(2,1)S(1)} all-gather(bf16[1,128,256]{2,1,0:T(8,128)(2,1)S(1)} %fusion.24), channel_id=2, replica_groups=mesh['row'=8,'col'=4] {'col'}, dimensions={1}, use_global_device_ids=true | all-gather | bytes 327680 | tf_op jit(solution)/shard_map/all_gather | solution.py:284
  42.2 0.7 fusion.44
  43.0 1.8 fusion.4
  44.8 24.8 %all-to-all-done = bf16[32,128,256]{2,1,0:T(8,128)(2,1)S(1)} async-done(((bf16[32,128,256]{2,1,0:T(8,128)(2,1)}), bf16[32,128,256]{2,1,0:T(8,128)(2,1)S(1)}, u32[]{:S(2)}, u32[]{:S(2)}) %all-to-all-start) | async-done | bytes 2097184 | tf_op jit(solution)/shard_map/all_to_all | solution.py:270
  69.5 0.6 gather_fusion.3
  70.2 1.3 multiply_reduce_fusion
  71.4 1.4 fusion
  72.9 0.1 copy-done.4
  73.0 0.6 fusion.6
  73.6 0.0 copy-start.8
  73.6 1.5 fusion.8
  75.1 0.8 fusion.11
  75.9 0.8 reshape.314
  76.7 0.0 all-gather.4.cloned.1.call-update
  76.8 0.0 reduce-scatter.3.cloned.1.call-start
  76.8 26.4 %all-gather.4.cloned.1.call-done = bf16[512,1024]{1,0:T(8,128)(2,1)} async-done(((bf16[128,1024]{1,0:T(8,128)(2,1)}), bf16[512,1024]{1,0:T(8,128)(2,1)}) %all-gather.4.cloned.1.call-update) | async-done | bytes 1048592 | tf_op jit(solution)/shard_map/all_gather | solution.py:299
  103.2 6.2 %convolution_convert_fusion = bf16[512,2048]{1,0:T(8,128)(2,1)} fusion(bf16[512,1024]{1,0:T(8,128)(2,1)} %all-gather.4.cloned.1.call-done, bf16[1024,2048]{1,0:T(8,128)(2,1)} %param.18), kind=kOutput, calls=%fused_computation.9 | convolution fusion | flops 2148532224 | bytes 7340032 | tf_op jit(solution)/shard_map/dot_general | solution.py:301
  109.4 0.0 reduce-scatter.3.cloned.1.call-update
  109.4 0.0 all-gather.6.cloned.1.call-start
  109.5 0.6 copy-done.12
  110.1 35.5 %reduce-scatter.3.cloned.1.call-done = bf16[64,2048]{1,0:T(8,128)(2,1)} async-done(((bf16[512,2048]{1,0:T(8,128)(2,1)}), bf16[64,2048]{1,0:T(8,128)(2,1)}) %reduce-scatter.3.cloned.1.call-update) | async-done | bytes 262160 | tf_op jit(solution)/shard_map/reduce_scatter | solution.py:300
  145.6 1.2 multiply_reduce_fusion.1
  146.8 0.1 copy.16
  146.9 0.1 copy.15
  147.0 0.1 copy.17
  147.2 0.8 concatenate.18
  148.0 0.0 all-gather.6.cloned.1.call-update
  148.0 0.2 reduce-scatter.5.cloned.1.call-start
  148.2 28.8 %all-gather.6.cloned.1.call-done.pieces_ref = bf16[512,2176]{1,0:T(8,128)(2,1)} async-done(((bf16[64,2176]{1,0:T(8,128)(2,1)}), bf16[512,2176]{1,0:T(8,128)(2,1)}) %all-gather.6.cloned.1.call-update) | async-done | bytes 2228240 | tf_op jit(solution)/shard_map/all_gather | solution.py:316
  177.0 1.0 convert_reduce_fusion
  178.0 0.1 broadcast_in_dim.51.squares_ref
  178.2 1.6 copy-done.3
  179.8 126.5 %shard_map.118 = bf16[4,128,2048]{2,1,0:T(8,128)(2,1)S(1)} custom-call(bf16[512,2176]{1,0:T(8,128)(2,1)S(1)} %copy-done.3, f32[4,128,128]{2,1,0:T(8,128)S(1)} %broadcast_in_dim.51.squares_ref, bf16[2048,3584]{1,0:T(8,128)(2,1)} %gate_ref.1, bf16[2048,3584]{1,0:T(8,128)(2,1)} %up_ref.1, bf16[3584,2048]{1,0:T(8,128)(2,1)} %down_ref.1), custom_call_target="tpu_custom_call" | custom-call | tf_op jit(solution)/shard_map/pallas_call | solution.py:202
  306.3 0.0 copy-start.2
  306.3 1.3 copy-done.2
  307.7 0.0 reduce-scatter.5.cloned.1.call-update
  307.7 35.4 %reduce-scatter.5.cloned.1.call-done = bf16[64,2048]{1,0:T(8,128)(2,1)} async-done(((bf16[512,2048]{1,0:T(8,128)(2,1)}), bf16[64,2048]{1,0:T(8,128)(2,1)}) %reduce-scatter.5.cloned.1.call-update) | async-done | bytes 262160 | tf_op jit(solution)/shard_map/reduce_scatter | solution.py:320
  343.1 1.7 add_convert_fusion
  (31 shorter events, 0.2 us)
Async XLA Ops:
  6.5 1.8 copy-start
  13.5 7.4 %copy-start.9 = (bf16[128,1024]{1,0:T(8,128)(2,1)S(1)}, bf16[128,1024]{1,0:T(8,128)(2,1)}, u32[]{:S(2)}) copy-start(bf16[128,1024]{1,0:T(8,128)(2,1)} %param.12) | copy-start | bytes 786436
  13.5 7.5 %copy-start.10 = (bf16[8,128,128]{2,1,0:T(8,128)(2,1)S(1)}, bf16[8,128,128]{2,1,0:T(8,128)(2,1)}, u32[]{:S(2)}) copy-start(bf16[8,128,128]{2,1,0:T(8,128)(2,1)} %param.15) | copy-start | bytes 786436
  13.5 7.6 %copy-start.11 = (bf16[8,128,128]{2,1,0:T(8,128)(2,1)S(1)}, bf16[8,128,128]{2,1,0:T(8,128)(2,1)}, u32[]{:S(2)}) copy-start(bf16[8,128,128]{2,1,0:T(8,128)(2,1)} %param.16) | copy-start | bytes 786436
  13.5 56.0 %all-to-all-start = ((bf16[32,128,256]{2,1,0:T(8,128)(2,1)}), bf16[32,128,256]{2,1,0:T(8,128)(2,1)S(1)}, u32[]{:S(2)}, u32[]{:S(2)}) async-start(bf16[32,128,256]{2,1,0:T(8,128)(2,1)} %maximum_select_fusion), calls=%async_computation | async-start | bytes 4194304 | tf_op jit(solution)/shard_map/all_to_all | solution.py:270
  20.9 82.4 %all-gather.4.cloned.1.call-start = ((), (), s32[]{:S(2)}) async-start(), calls=%async_computation.3 | async-start | bytes 1310720 | tf_op jit(solution)/shard_map/all_gather | solution.py:299
  42.2 0.7 copy-start.7
  71.4 1.6 copy-start.4
  73.6 1.5 copy-start.8
  76.8 68.9 %reduce-scatter.3.cloned.1.call-start = ((), (), s32[]{:S(2)}) async-start(), calls=%async_computation.4 | async-start | bytes 2359296 | tf_op jit(solution)/shard_map/reduce_scatter | solution.py:300
  109.4 0.7 copy-start.12
  109.4 36.2 %copy-start.5 = (bf16[64,2048]{1,0:T(8,128)(2,1)S(1)}, bf16[64,2048]{1,0:T(8,128)(2,1)}, u32[]{:S(2)}) copy-start(bf16[64,2048]{1,0:T(8,128)(2,1)} %param.19) | copy-start | bytes 786436
  109.4 67.6 %all-gather.6.cloned.1.call-start = ((), (), s32[]{:S(2)}) async-start(), calls=%async_computation.5 | async-start | bytes 2506752 | tf_op jit(solution)/shard_map/all_gather | solution.py:316
  148.0 195.1 %reduce-scatter.5.cloned.1.call-start = ((), (), s32[]{:S(2)}) async-start(), calls=%async_computation.6 | async-start | bytes 2359296 | tf_op jit(solution)/shard_map/reduce_scatter | solution.py:320
  178.2 1.6 copy-start.3
  179.8 165.0 %copy-start.1 = (bf16[8,1024,128]{2,1,0:T(8,128)(2,1)S(1)}, bf16[8,1024,128]{2,1,0:T(8,128)(2,1)}, u32[]{:S(2)}) copy-start(bf16[8,1024,128]{2,1,0:T(8,128)(2,1)} %param.13) | copy-start | bytes 6291460
  306.3 1.3 copy-start.2
  307.6 35.4 %copy-start.6 = (bf16[64,2048]{1,0:T(8,128)(2,1)S(1)}, bf16[64,2048]{1,0:T(8,128)(2,1)}, u32[]{:S(2)}) copy-start(bf16[64,2048]{1,0:T(8,128)(2,1)} %reduce-scatter.3.cloned.1.call-done) | copy-start | bytes 786436
Sparse Core Ops, SparseCore 0:
  76.9 26.3 all-gather.3
  109.6 36.0 reduce-scatter.2
  148.1 28.8 all-gather.5
  307.8 35.2 reduce-scatter.4

commit v3 on v2

--- a/solution.py
+++ b/solution.py
@@ -14,7 +14,7 @@
 BLK = 128
 GROUP = 8
 WIDTH = 256
-SLOTS = 3
+SLOTS = 4
 MESH = pl.DeviceIdType.MESH
 
 
@@ -30,58 +30,84 @@
     gate_buf,
     up_buf,
     down_buf,
-    part_buf,
-    sums_buf,
-    hidden_buf,
+    gate_part,
+    up_part,
+    gate_first,
+    up_first,
+    gate_mid,
+    up_mid,
+    gate_second,
+    up_second,
+    left,
+    right,
     square_buf,
     factor_buf,
     total,
     gate_sem,
     up_sem,
     down_sem,
-    sums_send,
-    sums_recv,
-    hidden_send,
-    hidden_recv,
+    pair_send,
+    pair_recv,
+    line_send,
+    line_recv,
     square_send,
     square_recv,
 ):
     me = lax.axis_index("col")
     depth = gate_ref.shape[0]
-
-    def target(k):
-        return lax.rem(me + k, peers)
-
-    def sums_copy(j, k):
-        slot = lax.rem(j, SLOTS)
+    lines = peers // 2
+    half = WIDTH // 2
+    pair_me = lax.rem(me, 2)
+    line_me = me // 2
+    other = line_me * 2 + (1 - pair_me)
+
+    def line(k):
+        return lax.rem(line_me + k, lines)
+
+    def remote(src, dst, send, recv, device):
         return pltpu.make_async_remote_copy(
-            src_ref=part_buf.at[slot, target(k)],
-            dst_ref=sums_buf.at[slot, k - 1],
-            send_sem=sums_send.at[slot, k - 1],
-            recv_sem=sums_recv.at[slot, k - 1],
-            device_id={"col": target(k)},
+            src_ref=src,
+            dst_ref=dst,
+            send_sem=send,
+            recv_sem=recv,
+            device_id={"col": device},
             device_id_type=MESH,
         )
 
-    def hidden_copy(j, k):
-        slot = lax.rem(j, SLOTS)
-        return pltpu.make_async_remote_copy(
-            src_ref=hidden_buf.at[slot, 0],
-            dst_ref=hidden_buf.at[slot, k],
-            send_sem=hidden_send.at[slot, k - 1],
-            recv_sem=hidden_recv.at[slot, k - 1],
-            device_id={"col": target(k)},
-            device_id_type=MESH,
-        )
+    def transfers(stage, slot):
+        if stage == 0:
+            pair = (gate_part.at[slot, 1 - pair_me], gate_first.at[slot])
+            along = [(up_part.at[slot, line(k)], up_first.at[slot, k - 1]) for k in range(1, lines)]
+        elif stage == 1:
+            pair = (up_mid.at[slot, 1 - pair_me], up_second.at[slot])
+            along = [(gate_mid.at[slot, line(k)], gate_second.at[slot, k - 1]) for k in range(1, lines)]
+        elif stage == 2:
+            pair = (left.at[slot, 0, 0], left.at[slot, 0, 1])
+            along = [(right.at[slot, 0, 0], right.at[slot, 0, k]) for k in range(1, lines)]
+        else:
+            pair = (right.at[slot, 0], right.at[slot, 1])
+            along = [(left.at[slot, 0], left.at[slot, k]) for k in range(1, lines)]
+        copies = [
+            remote(*pair, pair_send.at[stage, slot], pair_recv.at[stage, slot], other)
+        ]
+        for k in range(1, lines):
+            copies.append(
+                remote(
+                    *along[k - 1],
+                    line_send.at[stage, slot, k - 1],
+                    line_recv.at[stage, slot, k - 1],
+                    line(k) * 2 + pair_me,
+                )
+            )
+        return copies
 
     def square_copy(k):
-        return pltpu.make_async_remote_copy(
-            src_ref=squares_ref.at[target(k)],
-            dst_ref=square_buf.at[k - 1],
-            send_sem=square_send.at[k - 1],
-            recv_sem=square_recv.at[k - 1],
-            device_id={"col": target(k)},
-            device_id_type=MESH,
+        return remote(
+            squares_ref.at[lax.rem(me + k, peers)],
+            square_buf.at[k - 1],
+            square_send.at[k - 1],
+            square_recv.at[k - 1],
+            lax.rem(me + k, peers),
         )
 
     def columns(j):
@@ -108,14 +134,19 @@
     down_copy(0).start()
     barrier = pltpu.get_barrier_semaphore()
     for k in range(1, peers):
-        pl.semaphore_signal(barrier, inc=1, device_id={"col": target(k)}, device_id_type=MESH)
+        pl.semaphore_signal(
+            barrier, inc=1, device_id={"col": lax.rem(me + k, peers)}, device_id_type=MESH
+        )
     pl.semaphore_wait(barrier, peers - 1)
     for k in range(1, peers):
         square_copy(k).start()
     total[...] = jnp.zeros_like(total)
 
+    def stage_when(i, stage):
+        return pl.when((i >= stage) & (i < chunks + stage))
+
     def step(i, carry):
-        @pl.when(i < chunks)
+        @stage_when(i, 0)
         def _():
             @pl.when(i + 1 < chunks)
             def _():
@@ -123,20 +154,37 @@
                 up_copy(i + 1).start()
 
             slot = lax.rem(i, SLOTS)
-            for position, (copy, buf) in enumerate(((gate_copy, gate_buf), (up_copy, up_buf))):
-                copy(i).wait()
-                product = jnp.dot(
-                    pieces_ref[:, :depth],
-                    buf[lax.rem(i, 2)],
-                    preferred_element_type=jnp.float32,
-                ).astype(jnp.bfloat16)
-                part_buf[slot, :, :, position * WIDTH : (position + 1) * WIDTH] = product.reshape(
-                    peers, BLK, WIDTH
-                )
-            for k in range(1, peers):
-                sums_copy(i, k).start()
-
-        @pl.when(i == 1)
+            gate_copy(i).wait()
+            product = jnp.dot(
+                pieces_ref[:, :depth], gate_buf[lax.rem(i, 2)], preferred_element_type=jnp.float32
+            ).astype(jnp.bfloat16)
+            for b in range(peers):
+                gate_part[slot, b % 2, b // 2] = product[b * BLK : (b + 1) * BLK]
+            up_copy(i).wait()
+            product = jnp.dot(
+                pieces_ref[:, :depth], up_buf[lax.rem(i, 2)], preferred_element_type=jnp.float32
+            ).astype(jnp.bfloat16)
+            for b in range(peers):
+                up_part[slot, b // 2, b % 2] = product[b * BLK : (b + 1) * BLK]
+            for copy in transfers(0, slot):
+                copy.start()
+
+        @stage_when(i, 1)
+        def _():
+            slot = lax.rem(i - 1, SLOTS)
+            for copy in transfers(0, slot):
+                copy.wait()
+            gate_mid[slot] = (
+                gate_part[slot, pair_me].astype(jnp.float32) + gate_first[slot].astype(jnp.float32)
+            ).astype(jnp.bfloat16)
+            up_sum = up_part[slot, line_me].astype(jnp.float32)
+            for k in range(1, lines):
+                up_sum = up_sum + up_first[slot, k - 1].astype(jnp.float32)
+            up_mid[slot] = up_sum.astype(jnp.bfloat16)
+            for copy in transfers(1, slot):
+                copy.start()
+
+        @pl.when(i == 2)
         def _():
             squares = squares_ref[me]
             for k in range(1, peers):
@@ -144,25 +192,34 @@
                 squares = squares + square_buf[k - 1]
             factor_buf[...] = lax.rsqrt(squares / D + 1e-05)
 
-        @pl.when((i >= 1) & (i < chunks + 1))
-        def _():
-            j = i - 1
-            slot = lax.rem(j, SLOTS)
-            summed = part_buf[slot, me].astype(jnp.float32)
-            for k in range(1, peers):
-                sums_copy(j, k).wait()
-                summed = summed + sums_buf[slot, k - 1].astype(jnp.float32)
-            summed = summed * factor_buf[:, :1]
-            gate = summed[:, :WIDTH]
-            hidden_buf[slot, 0] = (
-                gate / (1.0 + jnp.exp(-gate)) * summed[:, WIDTH:]
-            ).astype(jnp.bfloat16)
-            for k in range(1, peers):
-                hidden_copy(j, k).start()
-
-        @pl.when(i >= 2)
-        def _():
-            j = i - 2
+        @stage_when(i, 2)
+        def _():
+            slot = lax.rem(i - 2, SLOTS)
+            for copy in transfers(1, slot):
+                copy.wait()
+            gate = gate_mid[slot, line_me].astype(jnp.float32)
+            for k in range(1, lines):
+                gate = gate + gate_second[slot, k - 1].astype(jnp.float32)
+            up = up_mid[slot, pair_me].astype(jnp.float32) + up_second[slot].astype(jnp.float32)
+            factor = factor_buf[:, :1]
+            gate = gate * factor
+            hidden = (gate / (1.0 + jnp.exp(-gate)) * (up * factor)).astype(jnp.bfloat16)
+            left[slot, 0, 0] = hidden[:, :half]
+            right[slot, 0, 0] = hidden[:, half:]
+            for copy in transfers(2, slot):
+                copy.start()
+
+        @stage_when(i, 3)
+        def _():
+            slot = lax.rem(i - 3, SLOTS)
+            for copy in transfers(2, slot):
+                copy.wait()
+            for copy in transfers(3, slot):
+                copy.start()
+
+        @stage_when(i, 4)
+        def _():
+            j = i - 4
             slot = lax.rem(j, SLOTS)
 
             @pl.when(j + 1 < chunks)
@@ -170,9 +227,16 @@
                 down_copy(j + 1).start()
 
             down_copy(j).wait()
-            for k in range(1, peers):
-                hidden_copy(j, k).wait()
-            gathered = hidden_buf[slot].reshape(peers * BLK, WIDTH)
+            for copy in transfers(3, slot):
+                copy.wait()
+            gathered = jnp.concatenate(
+                [
+                    jnp.concatenate([left[slot, k, p], right[slot, p, k]], axis=1)
+                    for p in range(2)
+                    for k in range(lines)
+                ],
+                axis=0,
+            )
             out_width = total.shape[1]
             tile = min(512, out_width)
             for start in range(0, out_width, tile):
@@ -184,43 +248,56 @@
 
         return carry
 
-    lax.fori_loop(0, chunks + 2, step, 0)
-    for k in range(peers):
-        owner = lax.rem(me + peers - k, peers)
-        out_ref[owner] = total[k * BLK : (k + 1) * BLK, :].astype(jnp.bfloat16)
+    lax.fori_loop(0, chunks + 4, step, 0)
+    for p in range(2):
+        for k in range(lines):
+            owner = line(lines - k) * 2 + lax.rem(pair_me + p, 2)
+            first = (p * lines + k) * BLK
+            out_ref[owner] = total[first : first + BLK, :].astype(jnp.bfloat16)
 
 
 def feed_forward(pieces, squares, gate_weight, up_weight, down_weight):
     peers = lax.axis_size("col")
+    lines = peers // 2
     depth, hidden_width = gate_weight.shape
     out_width = down_weight.shape[1]
     chunks = hidden_width // WIDTH
     vmem = pl.BlockSpec(memory_space=pltpu.VMEM)
     hbm = pl.BlockSpec(memory_space=pl.ANY)
-    pair = (SLOTS, peers - 1)
     dma = pltpu.SemaphoreType.DMA
+
+    def held(*shape):
+        return pltpu.VMEM(shape, jnp.bfloat16)
+
     return pl.pallas_call(
         functools.partial(feed_forward_kernel, peers, chunks),
         out_shape=jax.ShapeDtypeStruct((peers, BLK, out_width), jnp.bfloat16),
         in_specs=[vmem, vmem, hbm, hbm, hbm],
         out_specs=vmem,
         scratch_shapes=[
-            pltpu.VMEM((2, depth, WIDTH), jnp.bfloat16),
-            pltpu.VMEM((2, depth, WIDTH), jnp.bfloat16),
-            pltpu.VMEM((2, WIDTH, out_width), jnp.bfloat16),
-            pltpu.VMEM((SLOTS, peers, BLK, 2 * WIDTH), jnp.bfloat16),
-            pltpu.VMEM((SLOTS, peers - 1, BLK, 2 * WIDTH), jnp.bfloat16),
-            pltpu.VMEM((SLOTS, peers, BLK, WIDTH), jnp.bfloat16),
+            held(2, depth, WIDTH),
+            held(2, depth, WIDTH),
+            held(2, WIDTH, out_width),
+            held(SLOTS, 2, lines, BLK, WIDTH),
+            held(SLOTS, lines, 2, BLK, WIDTH),
+            held(SLOTS, lines, BLK, WIDTH),
+            held(SLOTS, lines - 1, 2, BLK, WIDTH),
+            held(SLOTS, lines, BLK, WIDTH),
+            held(SLOTS, 2, BLK, WIDTH),
+            held(SLOTS, lines - 1, BLK, WIDTH),
+            held(SLOTS, BLK, WIDTH),
+            held(SLOTS, lines, 2, BLK, WIDTH // 2),
+            held(SLOTS, 2, lines, BLK, WIDTH // 2),
             pltpu.VMEM((peers - 1, BLK, 128), jnp.float32),
             pltpu.VMEM((BLK, 128), jnp.float32),
             pltpu.VMEM((peers * BLK, out_width), jnp.float32),
             dma((2,)),
             dma((2,)),
             dma((2,)),
-            dma(pair),
-            dma(pair),
-            dma(pair),
-            dma(pair),
+            dma((4, SLOTS)),
+            dma((4, SLOTS)),
+            dma((4, SLOTS, lines - 1)),
+            dma((4, SLOTS, lines - 1)),
             dma((peers - 1,)),
             dma((peers - 1,)),
         ],
@@ -228,6 +305,67 @@
             collective_id=0, has_side_effects=True, vmem_limit_bytes=48 * 1024 * 1024
         ),
     )(pieces, squares, gate_weight, up_weight, down_weight)
+
+
+def project_kernel(peers, own_ref, weight_ref, out_ref, gathered, weight_buf, weight_sem, send, recv):
+    me = lax.axis_index("col")
+
+    def copy_to(k):
+        return pltpu.make_async_remote_copy(
+            src_ref=own_ref,
+            dst_ref=gathered.at[k - 1],
+            send_sem=send.at[k - 1],
+            recv_sem=recv.at[k - 1],
+            device_id={"col": lax.rem(me + k, peers)},
+            device_id_type=MESH,
+        )
+
+    weights = pltpu.make_async_copy(weight_ref, weight_buf, weight_sem)
+    weights.start()
+    barrier = pltpu.get_barrier_semaphore()
+    for k in range(1, peers):
+        pl.semaphore_signal(
+            barrier, inc=1, device_id={"col": lax.rem(me + k, peers)}, device_id_type=MESH
+        )
+    pl.semaphore_wait(barrier, peers - 1)
+    for k in range(1, peers):
+        copy_to(k).start()
+    weights.wait()
+    out_width = weight_buf.shape[1]
+    tile = min(512, out_width)
+    for k in range(peers):
+        if k > 0:
+            copy_to(k).wait()
+            rows = gathered[k - 1]
+        else:
+            rows = own_ref[...]
+        owner = lax.rem(me + peers - k, peers)
+        for start in range(0, out_width, tile):
+            out_ref[owner, :, start : start + tile] = jnp.dot(
+                rows, weight_buf[:, start : start + tile], preferred_element_type=jnp.float32
+            ).astype(jnp.bfloat16)
+
+
+def project(attended, out_weight):
+    peers = lax.axis_size("col")
+    width, out_width = out_weight.shape
+    dma = pltpu.SemaphoreType.DMA
+    return pl.pallas_call(
+        functools.partial(project_kernel, peers),
+        out_shape=jax.ShapeDtypeStruct((peers, BLK, out_width), jnp.bfloat16),
+        in_specs=[pl.BlockSpec(memory_space=pltpu.VMEM), pl.BlockSpec(memory_space=pl.ANY)],
+        out_specs=pl.BlockSpec(memory_space=pltpu.VMEM),
+        scratch_shapes=[
+            pltpu.VMEM((peers - 1, BLK, width), jnp.bfloat16),
+            pltpu.VMEM((width, out_width), jnp.bfloat16),
+            dma,
+            dma((peers - 1,)),
+            dma((peers - 1,)),
+        ],
+        compiler_params=pltpu.CompilerParams(
+            collective_id=1, has_side_effects=True, vmem_limit_bytes=48 * 1024 * 1024
+        ),
+    )(attended, out_weight)
 
 
 def local(
@@ -296,9 +434,8 @@
         weights.astype(jnp.bfloat16), piece_values, preferred_element_type=jnp.float32
     )
     attended = (new_acc / new_sum[:, None]).astype(jnp.bfloat16).reshape(BLK, heads_here * HEAD_DIM)
-    all_attended = lax.all_gather(attended, "col", axis=0, tiled=True)
     projected = lax.psum_scatter(
-        jnp.dot(all_attended, out_weight, preferred_element_type=jnp.float32).astype(jnp.bfloat16),
+        project(attended, out_weight).reshape(-1, out_weight.shape[1]),
         "row",
         scatter_dimension=0,
         tiled=True,

time: 352 us -> 307 us (0.87)
  waiting for transfers between devices: 151 us -> 123 us
  Pallas kernels: 127 us -> 116 us
  matrix products: 11.5 us -> 5.29 us
    pallas_call x1, Pallas kernels: 127 us -> 99 us  [feed_forward(): pl.pallas_call(functools.partial(feed_forward_kernel, peers, chunks), out...]
    all_gather x1 -> x0, waiting for transfers between devices: 26.4 us -> none  [local(): all_attended = lax.all_gather(attended, 'col', axis=0, tiled=True)]
    pallas_call x0 -> x1, Pallas kernels: none -> 17.3 us  [project(): pl.pallas_call(functools.partial(project_kernel, peers), out_shape=jax.Sh...]
    dot_general x1 -> x0, matrix products: 6.18 us -> none  [local(): jnp.dot(all_attended, out_weight, preferred_element_type=jnp.float32)]
  transfers between devices with their start and end apart: 5 -> 4, of which waited for: 5 -> 4; matrix products, arithmetic and copies ran while one was open for 1% -> 1% of each run, Pallas kernels for 0% -> 0%
where the time goes in v3:
time: 307 us
  waiting for transfers between devices  123 us (40%)
  Pallas kernels  116 us (38%)
  blocking collectives  21.1 us (7%)
  between operations  13.4 us (4%)
  local copies, waits for them, and re-layouts  10.4 us (3%)
  other arithmetic  9.06 us (3%)
  starting transfers between devices  7.63 us (2%)
  matrix products  5.29 us (2%)
    pallas_call x1, Pallas kernels, feed_forward(): pl.pallas_call(functools.partial(feed_forward_kernel, peers, chunks), out...  99 us
    reduce_scatter x1, waiting for transfers between devices, local(): lax.psum_scatter(project(attended, out_weight).reshape(-1, out_weight.sha...  35.1 us
    reduce_scatter x1, waiting for transfers between devices, local(): lax.psum_scatter(down_terms.reshape(-1, down_terms.shape[2]), 'row', scat...  34.7 us
    all_gather x1, waiting for transfers between devices, local(): pieces = lax.all_gather(outgoing_piece, 'row', axis=0, tiled=True)  28.7 us
    all_to_all x1, waiting for transfers between devices, local(): lax.all_to_all(outgoing, ('row', 'col'), split_axis=0, concat_axis=0, til...  24.8 us
    all_gather x1, blocking collectives, local(): piece = lax.all_gather(own, 'col', axis=0, tiled=True)  21.1 us
    pallas_call x1, Pallas kernels, project(): pl.pallas_call(functools.partial(project_kernel, peers), out_shape=jax.Sh...  17.3 us
    all_to_all x1, starting transfers between devices, local(): lax.all_to_all(outgoing, ('row', 'col'), split_axis=0, concat_axis=0, til...  7.33 us
  transfers between devices with their start and end apart: 4, of which 4 were waited for; matrix products, arithmetic and copies ran while one was open for 1% of the time, Pallas kernels for 0%

profile of v3, /device:TPU:0, one launch (start us, length us, event | category | flops | bytes accessed | tf_op | source)
XLA Modules:
  0.0 306.5 jit_solution(12815740741344969028)
XLA Ops:
  6.5 0.0 copy-start
  6.6 1.5 gather_fusion
  8.1 0.1 fusion.51
  8.2 0.1 fusion.29
  8.4 0.0 copy-done
  8.4 0.7 gather_fusion.1
  9.1 2.3 gather_fusion.2
  11.5 2.0 maximum_select_fusion
  13.5 7.3 %all-to-all-start = ((bf16[32,128,256]{2,1,0:T(8,128)(2,1)}), bf16[32,128,256]{2,1,0:T(8,128)(2,1)S(1)}, u32[]{:S(2)}, u32[]{:S(2)}) async-start(bf16[32,128,256]{2,1,0:T(8,128)(2,1)} %maximum_select_fusion), calls=%async_computation | async-start | bytes 4194304 | tf_op jit(solution)/shard_map/all_to_all | solution.py:408
  20.9 0.0 reduce-scatter.3.cloned.1.call-start
  20.9 0.0 copy-done.9
  21.0 0.1 reshape.316
  21.1 21.1 %all-gather = bf16[1,512,256]{2,1,0:T(8,128)(2,1)S(1)} all-gather(bf16[1,128,256]{2,1,0:T(8,128)(2,1)S(1)} %fusion.24), channel_id=2, replica_groups=mesh['row'=8,'col'=4] {'col'}, dimensions={1}, use_global_device_ids=true | all-gather | bytes 327680 | tf_op jit(solution)/shard_map/all_gather | solution.py:422
  42.2 0.7 fusion.44
  43.0 1.8 fusion.4
  44.8 24.8 %all-to-all-done = bf16[32,128,256]{2,1,0:T(8,128)(2,1)S(1)} async-done(((bf16[32,128,256]{2,1,0:T(8,128)(2,1)}), bf16[32,128,256]{2,1,0:T(8,128)(2,1)S(1)}, u32[]{:S(2)}, u32[]{:S(2)}) %all-to-all-start) | async-done | bytes 2097184 | tf_op jit(solution)/shard_map/all_to_all | solution.py:408
  69.6 0.6 gather_fusion.3
  70.2 1.2 multiply_reduce_fusion
  71.4 1.4 fusion
  72.9 0.1 copy-done.4
  73.0 0.6 fusion.6
  73.6 0.0 copy-start.8
  73.6 1.5 fusion.8
  75.1 0.8 fusion.11
  75.9 0.1 reshape.317.own_ref
  76.1 17.3 %shard_map.118 = bf16[4,128,2048]{2,1,0:T(8,128)(2,1)} custom-call(bf16[128,1024]{1,0:T(8,128)(2,1)S(1)} %reshape.317.own_ref, bf16[1024,2048]{1,0:T(8,128)(2,1)} %weight_ref.1), custom_call_target="tpu_custom_call" | custom-call | tf_op jit(solution)/shard_map/pallas_call | solution.py:353
  93.3 0.0 copy-start.12
  93.4 0.0 copy-start.5
  93.4 0.0 reduce-scatter.3.cloned.1.call-update
  93.4 0.0 all-gather.3.cloned.1.call-start
  93.4 0.6 copy-done.12
  94.0 35.1 %reduce-scatter.3.cloned.1.call-done = bf16[64,2048]{1,0:T(8,128)(2,1)} async-done(((bf16[512,2048]{1,0:T(8,128)(2,1)}), bf16[64,2048]{1,0:T(8,128)(2,1)}) %reduce-scatter.3.cloned.1.call-update) | async-done | bytes 262160 | tf_op jit(solution)/shard_map/reduce_scatter | solution.py:437
  129.1 1.2 multiply_reduce_fusion.1
  130.3 0.1 copy.16
  130.4 0.1 copy.15
  130.5 0.1 copy.17
  130.6 0.8 concatenate.18
  131.4 0.0 all-gather.3.cloned.1.call-update
  131.5 0.2 reduce-scatter.5.cloned.1.call-start
  131.7 28.7 %all-gather.3.cloned.1.call-done.pieces_ref = bf16[512,2176]{1,0:T(8,128)(2,1)} async-done(((bf16[64,2176]{1,0:T(8,128)(2,1)}), bf16[512,2176]{1,0:T(8,128)(2,1)}) %all-gather.3.cloned.1.call-update) | async-done | bytes 2228240 | tf_op jit(solution)/shard_map/all_gather | solution.py:453
  160.4 1.0 convert_reduce_fusion
  161.4 0.1 broadcast_in_dim.51.squares_ref
  161.6 1.6 copy-done.3
  163.2 99.0 %shard_map.119 = bf16[4,128,2048]{2,1,0:T(8,128)(2,1)S(1)} custom-call(bf16[512,2176]{1,0:T(8,128)(2,1)S(1)} %copy-done.3, f32[4,128,128]{2,1,0:T(8,128)S(1)} %broadcast_in_dim.51.squares_ref, bf16[2048,3584]{1,0:T(8,128)(2,1)} %gate_ref.1, bf16[2048,3584]{1,0:T(8,128)(2,1)} %up_ref.1, bf16[3584,2048]{1,0:T(8,128)(2,1)} %down_ref.1), custom_call_target="tpu_custom_call" | custom-call | tf_op jit(solution)/shard_map/pallas_call | solution.py:272
  262.2 1.3 copy-done.2
  263.5 0.0 reduce-scatter.5.cloned.1.call-update
  263.6 34.7 %reduce-scatter.5.cloned.1.call-done = bf16[64,2048]{1,0:T(8,128)(2,1)} async-done(((bf16[512,2048]{1,0:T(8,128)(2,1)}), bf16[64,2048]{1,0:T(8,128)(2,1)}) %reduce-scatter.5.cloned.1.call-update) | async-done | bytes 262160 | tf_op jit(solution)/shard_map/reduce_scatter | solution.py:457
  298.2 1.7 add_convert_fusion
  (28 shorter events, 0.2 us)
Async XLA Ops:
  6.5 1.8 copy-start
  13.5 7.4 %copy-start.9 = (bf16[128,1024]{1,0:T(8,128)(2,1)S(1)}, bf16[128,1024]{1,0:T(8,128)(2,1)}, u32[]{:S(2)}) copy-start(bf16[128,1024]{1,0:T(8,128)(2,1)} %param.12) | copy-start | bytes 786436
  13.5 7.5 %copy-start.10 = (bf16[8,128,128]{2,1,0:T(8,128)(2,1)S(1)}, bf16[8,128,128]{2,1,0:T(8,128)(2,1)}, u32[]{:S(2)}) copy-start(bf16[8,128,128]{2,1,0:T(8,128)(2,1)} %param.15) | copy-start | bytes 786436
  13.5 7.6 %copy-start.11 = (bf16[8,128,128]{2,1,0:T(8,128)(2,1)S(1)}, bf16[8,128,128]{2,1,0:T(8,128)(2,1)}, u32[]{:S(2)}) copy-start(bf16[8,128,128]{2,1,0:T(8,128)(2,1)} %param.16) | copy-start | bytes 786436
  13.5 56.0 %all-to-all-start = ((bf16[32,128,256]{2,1,0:T(8,128)(2,1)}), bf16[32,128,256]{2,1,0:T(8,128)(2,1)S(1)}, u32[]{:S(2)}, u32[]{:S(2)}) async-start(bf16[32,128,256]{2,1,0:T(8,128)(2,1)} %maximum_select_fusion), calls=%async_computation | async-start | bytes 4194304 | tf_op jit(solution)/shard_map/all_to_all | solution.py:408
  20.9 108.2 %reduce-scatter.3.cloned.1.call-start = ((), (), s32[]{:S(2)}) async-start(), calls=%async_computation.3 | async-start | bytes 2359296 | tf_op jit(solution)/shard_map/reduce_scatter | solution.py:437
  42.2 0.7 copy-start.7
  71.4 1.6 copy-start.4
  73.6 1.5 copy-start.8
  93.3 0.7 copy-start.12
  93.4 35.7 %copy-start.5 = (bf16[64,2048]{1,0:T(8,128)(2,1)S(1)}, bf16[64,2048]{1,0:T(8,128)(2,1)}, u32[]{:S(2)}) copy-start(bf16[64,2048]{1,0:T(8,128)(2,1)} %param.19) | copy-start | bytes 786436
  93.4 67.0 %all-gather.3.cloned.1.call-start = ((), (), s32[]{:S(2)}) async-start(), calls=%async_computation.4 | async-start | bytes 2506752 | tf_op jit(solution)/shard_map/all_gather | solution.py:453
  131.5 166.8 %reduce-scatter.5.cloned.1.call-start = ((), (), s32[]{:S(2)}) async-start(), calls=%async_computation.5 | async-start | bytes 2359296 | tf_op jit(solution)/shard_map/reduce_scatter | solution.py:457
  161.6 1.6 copy-start.3
  163.2 136.8 %copy-start.1 = (bf16[8,1024,128]{2,1,0:T(8,128)(2,1)S(1)}, bf16[8,1024,128]{2,1,0:T(8,128)(2,1)}, u32[]{:S(2)}) copy-start(bf16[8,1024,128]{2,1,0:T(8,128)(2,1)} %param.13) | copy-start | bytes 6291460
  262.2 1.3 copy-start.2
  263.5 34.7 %copy-start.6 = (bf16[64,2048]{1,0:T(8,128)(2,1)S(1)}, bf16[64,2048]{1,0:T(8,128)(2,1)}, u32[]{:S(2)}) copy-start(bf16[64,2048]{1,0:T(8,128)(2,1)} %reduce-scatter.3.cloned.1.call-done) | copy-start | bytes 786436
Sparse Core Ops, SparseCore 0:
  93.5 35.5 reduce-scatter.2
  131.6 28.7 all-gather.2
  263.7 34.5 reduce-scatter.4

commit v4 on v3

--- a/solution.py
+++ b/solution.py
@@ -366,6 +366,88 @@
             collective_id=1, has_side_effects=True, vmem_limit_bytes=48 * 1024 * 1024
         ),
     )(attended, out_weight)
+
+
+def row_sum_kernel(lines, part_ref, out_ref, first, mid, second, pair_send, pair_recv, line_send, line_recv):
+    me = lax.axis_index("row")
+    pair_me = lax.rem(me, 2)
+    line_me = me // 2
+    other = line_me * 2 + (1 - pair_me)
+    pieces, _, _, width = first.shape
+
+    def line(k):
+        return lax.rem(line_me + k, lines)
+
+    def pair_copy(c):
+        return pltpu.make_async_remote_copy(
+            src_ref=part_ref.at[:, 1 - pair_me, :, c * width : (c + 1) * width],
+            dst_ref=first.at[c],
+            send_sem=pair_send.at[c],
+            recv_sem=pair_recv.at[c],
+            device_id={"row": other},
+            device_id_type=MESH,
+        )
+
+    def line_copy(c, k):
+        return pltpu.make_async_remote_copy(
+            src_ref=mid.at[c, line(k)],
+            dst_ref=second.at[c, k - 1],
+            send_sem=line_send.at[c, k - 1],
+            recv_sem=line_recv.at[c, k - 1],
+            device_id={"row": line(k) * 2 + pair_me},
+            device_id_type=MESH,
+        )
+
+    barrier = pltpu.get_barrier_semaphore()
+    pl.semaphore_signal(barrier, inc=1, device_id={"row": other}, device_id_type=MESH)
+    for k in range(1, lines):
+        pl.semaphore_signal(
+            barrier, inc=1, device_id={"row": line(k) * 2 + pair_me}, device_id_type=MESH
+        )
+    pl.semaphore_wait(barrier, lines)
+    for c in range(pieces):
+        pair_copy(c).start()
+    for c in range(pieces):
+        pair_copy(c).wait()
+        own = part_ref[:, pair_me, :, c * width : (c + 1) * width]
+        mid[c] = (own.astype(jnp.float32) + first[c].astype(jnp.float32)).astype(jnp.bfloat16)
+        for k in range(1, lines):
+            line_copy(c, k).start()
+    for c in range(pieces):
+        result = mid[c, line_me].astype(jnp.float32)
+        for k in range(1, lines):
+            line_copy(c, k).wait()
+            result = result + second[c, k - 1].astype(jnp.float32)
+        out_ref[:, c * width : (c + 1) * width] = result
+
+
+def row_sum(partial, collective_id):
+    rows = lax.axis_size("row")
+    lines = rows // 2
+    width = partial.shape[-1]
+    tokens = partial.shape[0] * partial.shape[1] // rows
+    pieces = 4
+    part = width // pieces
+    vmem = pl.BlockSpec(memory_space=pltpu.VMEM)
+    dma = pltpu.SemaphoreType.DMA
+    return pl.pallas_call(
+        functools.partial(row_sum_kernel, lines),
+        out_shape=jax.ShapeDtypeStruct((tokens, width), jnp.float32),
+        in_specs=[vmem],
+        out_specs=vmem,
+        scratch_shapes=[
+            pltpu.VMEM((pieces, lines, tokens, part), jnp.bfloat16),
+            pltpu.VMEM((pieces, lines, tokens, part), jnp.bfloat16),
+            pltpu.VMEM((pieces, lines - 1, tokens, part), jnp.bfloat16),
+            dma((pieces,)),
+            dma((pieces,)),
+            dma((pieces, lines - 1)),
+            dma((pieces, lines - 1)),
+        ],
+        compiler_params=pltpu.CompilerParams(
+            collective_id=collective_id, has_side_effects=True, vmem_limit_bytes=32 * 1024 * 1024
+        ),
+    )(partial.reshape(lines, 2, tokens, width))
 
 
 def local(
@@ -434,12 +516,7 @@
         weights.astype(jnp.bfloat16), piece_values, preferred_element_type=jnp.float32
     )
     attended = (new_acc / new_sum[:, None]).astype(jnp.bfloat16).reshape(BLK, heads_here * HEAD_DIM)
-    projected = lax.psum_scatter(
-        project(attended, out_weight).reshape(-1, out_weight.shape[1]),
-        "row",
-        scatter_dimension=0,
-        tiled=True,
-    )
+    projected = row_sum(project(attended, out_weight), 2)
     stream = residual.astype(jnp.float32) + projected.astype(jnp.float32)
     scaled = (stream * norm_gain.astype(jnp.float32)).astype(jnp.bfloat16)
     rest = jnp.sum(stream * stream, axis=1, keepdims=True)
@@ -454,9 +531,7 @@
     squares = jnp.sum(pieces[:, scaled.shape[1] :].astype(jnp.float32), axis=1, keepdims=True)
     squares = jnp.broadcast_to(squares, (squares.shape[0], 128)).reshape(col_count, BLK, 128)
     down_terms = feed_forward(pieces, squares, gate_weight, up_weight, down_weight)
-    mlp_part = lax.psum_scatter(
-        down_terms.reshape(-1, down_terms.shape[2]), "row", scatter_dimension=0, tiled=True
-    )
+    mlp_part = row_sum(down_terms, 3)
     return (stream + mlp_part.astype(jnp.float32)).astype(jnp.bfloat16)
 
 

time: 307 us -> 289 us (0.941)
  waiting for transfers between devices: 123 us -> 55.7 us
  Pallas kernels: 116 us -> 169 us
    reduce_scatter x2 -> x0, waiting for transfers between devices: 69.7 us -> none  [the longest x1 35.1 us: local(): lax.psum_scatter(project(attended, out_weight).reshape(-1, out_weight.sha...]
    pallas_call x0 -> x2, Pallas kernels: none -> 54.5 us  [row_sum(): pl.pallas_call(functools.partial(row_sum_kernel, lines), out_shape=jax.Sh...]
  transfers between devices with their start and end apart: 4 -> 2, of which waited for: 4 -> 2; matrix products, arithmetic and copies ran while one was open for 1% -> 1% of each run, Pallas kernels for 0% -> 0%
where the time goes in v4:
time: 289 us; the launch traced here: 288 us
  Pallas kernels  169 us (58%)
  waiting for transfers between devices  55.7 us (19%)
  blocking collectives  21.1 us (7%)
  between operations  13.7 us (5%)
  local copies, waits for them, and re-layouts  8.52 us (3%)
  starting transfers between devices  7.37 us (3%)
  other arithmetic  7.13 us (2%)
  matrix products  5.29 us (2%)
    pallas_call x1, Pallas kernels, feed_forward(): pl.pallas_call(functools.partial(feed_forward_kernel, peers, chunks), out...  99 us
    pallas_call x2, Pallas kernels, row_sum(): pl.pallas_call(functools.partial(row_sum_kernel, lines), out_shape=jax.Sh...  54.5 us
    all_gather x1, waiting for transfers between devices, local(): pieces = lax.all_gather(outgoing_piece, 'row', axis=0, tiled=True)  30.9 us
    all_to_all x1, waiting for transfers between devices, local(): lax.all_to_all(outgoing, ('row', 'col'), split_axis=0, concat_axis=0, til...  24.8 us
    all_gather x1, blocking collectives, local(): piece = lax.all_gather(own, 'col', axis=0, tiled=True)  21.1 us
    pallas_call x1, Pallas kernels, project(): pl.pallas_call(functools.partial(project_kernel, peers), out_shape=jax.Sh...  15.9 us
    all_to_all x1, starting transfers between devices, local(): lax.all_to_all(outgoing, ('row', 'col'), split_axis=0, concat_axis=0, til...  7.33 us
  transfers between devices with their start and end apart: 2, of which 2 were waited for; matrix products, arithmetic and copies ran while one was open for 1% of the time, Pallas kernels for 0%

profile of v4, /device:TPU:0, one launch (start us, length us, event | category | flops | bytes accessed | tf_op | source)
XLA Modules:
  0.0 288.3 jit_solution(10123626797566761036)
XLA Ops:
  6.5 0.0 copy-start
  6.6 1.5 gather_fusion
  8.1 0.1 fusion.51
  8.2 0.1 fusion.29
  8.4 0.0 copy-done
  8.4 0.7 gather_fusion.1
  9.1 2.3 gather_fusion.2
  11.5 2.1 maximum_select_fusion
  13.6 7.3 %all-to-all-start = ((bf16[32,128,256]{2,1,0:T(8,128)(2,1)}), bf16[32,128,256]{2,1,0:T(8,128)(2,1)S(1)}, u32[]{:S(2)}, u32[]{:S(2)}) async-start(bf16[32,128,256]{2,1,0:T(8,128)(2,1)} %maximum_select_fusion), calls=%async_computation | async-start | bytes 4194304 | tf_op jit(solution)/shard_map/all_to_all | solution.py:490
  20.9 0.0 all-gather.3.cloned.1.call-start
  21.0 0.0 copy-done.7
  21.0 0.1 reshape.316
  21.1 0.0 copy-done.10
  21.1 0.0 copy-done.8
  21.1 0.0 copy-done.9
  21.2 21.1 %all-gather = bf16[1,512,256]{2,1,0:T(8,128)(2,1)S(1)} all-gather(bf16[1,128,256]{2,1,0:T(8,128)(2,1)S(1)} %fusion.24), channel_id=2, replica_groups=mesh['row'=8,'col'=4] {'col'}, dimensions={1}, use_global_device_ids=true | all-gather | bytes 327680 | tf_op jit(solution)/shard_map/all_gather | solution.py:504
  42.3 0.7 fusion.44
  43.0 0.0 copy-done.5
  43.0 1.8 fusion.4
  44.8 24.8 %all-to-all-done = bf16[32,128,256]{2,1,0:T(8,128)(2,1)S(1)} async-done(((bf16[32,128,256]{2,1,0:T(8,128)(2,1)}), bf16[32,128,256]{2,1,0:T(8,128)(2,1)S(1)}, u32[]{:S(2)}, u32[]{:S(2)}) %all-to-all-start) | async-done | bytes 2097184 | tf_op jit(solution)/shard_map/all_to_all | solution.py:490
  69.6 0.6 gather_fusion.3
  70.2 1.3 multiply_reduce_fusion
  71.5 0.0 copy-start.3
  71.5 1.4 fusion
  72.9 0.1 copy-done.3
  73.1 0.6 fusion.6
  73.7 0.0 copy-start.6
  73.7 1.5 fusion.8
  75.2 0.0 copy-done.6
  75.2 0.8 fusion.11
  76.0 0.1 reshape.317.own_ref
  76.1 15.9 %shard_map.118 = bf16[4,128,2048]{2,1,0:T(8,128)(2,1)S(1)} custom-call(bf16[128,1024]{1,0:T(8,128)(2,1)S(1)} %reshape.317.own_ref, bf16[1024,2048]{1,0:T(8,128)(2,1)} %weight_ref.1), custom_call_target="tpu_custom_call" | custom-call | tf_op jit(solution)/shard_map/pallas_call | solution.py:353
  92.0 0.0 copy-start.4
  92.0 27.3 %shard_map.119 = f32[64,2048]{1,0:T(8,128)S(1)} custom-call(bf16[4,2,64,2048]{3,2,1,0:T(8,128)(2,1)S(1)} %bitcast.42), custom_call_target="tpu_custom_call" | custom-call | tf_op jit(solution)/shard_map/pallas_call | solution.py:433
  119.3 0.2 multiply_reduce_fusion.1
  119.5 0.1 copy.16
  119.6 0.1 copy.15
  119.7 0.1 copy.17
  119.9 0.8 concatenate.18
  120.7 0.0 all-gather.3.cloned.1.call-update
  120.7 30.9 %all-gather.3.cloned.1.call-done.pieces_ref = bf16[512,2176]{1,0:T(8,128)(2,1)} async-done(((bf16[64,2176]{1,0:T(8,128)(2,1)}), bf16[512,2176]{1,0:T(8,128)(2,1)}) %all-gather.3.cloned.1.call-update) | async-done | bytes 2228240 | tf_op jit(solution)/shard_map/all_gather | solution.py:530
  151.6 1.0 convert_reduce_fusion
  152.6 0.1 broadcast_in_dim.51.squares_ref
  152.7 1.6 copy-done.2
  154.4 99.0 %shard_map.120 = bf16[4,128,2048]{2,1,0:T(8,128)(2,1)S(1)} custom-call(bf16[512,2176]{1,0:T(8,128)(2,1)S(1)} %copy-done.2, f32[4,128,128]{2,1,0:T(8,128)S(1)} %broadcast_in_dim.51.squares_ref, bf16[2048,3584]{1,0:T(8,128)(2,1)} %gate_ref.1, bf16[2048,3584]{1,0:T(8,128)(2,1)} %up_ref.1, bf16[3584,2048]{1,0:T(8,128)(2,1)} %down_ref.1), custom_call_target="tpu_custom_call" | custom-call | tf_op jit(solution)/shard_map/pallas_call | solution.py:272
  253.4 0.0 copy-start.1
  253.4 27.2 %shard_map.121 = f32[64,2048]{1,0:T(8,128)S(1)} custom-call(bf16[4,2,64,2048]{3,2,1,0:T(8,128)(2,1)S(1)} %bitcast.41), custom_call_target="tpu_custom_call" | custom-call | tf_op jit(solution)/shard_map/pallas_call | solution.py:433
  280.7 0.8 add_convert_fusion
  (20 shorter events, 0.1 us)
Async XLA Ops:
  6.5 1.8 copy-start
  13.6 7.4 %copy-start.7 = (bf16[128,1024]{1,0:T(8,128)(2,1)S(1)}, bf16[128,1024]{1,0:T(8,128)(2,1)}, u32[]{:S(2)}) copy-start(bf16[128,1024]{1,0:T(8,128)(2,1)} %param.12) | copy-start | bytes 786436
  13.6 7.5 %copy-start.10 = (bf16[2048]{0:T(1024)(128)(2,1)S(1)}, bf16[2048]{0:T(1024)(128)(2,1)}, u32[]{:S(2)}) copy-start(bf16[2048]{0:T(1024)(128)(2,1)} %param.20) | copy-start | bytes 12292
  13.6 7.6 %copy-start.8 = (bf16[8,128,128]{2,1,0:T(8,128)(2,1)S(1)}, bf16[8,128,128]{2,1,0:T(8,128)(2,1)}, u32[]{:S(2)}) copy-start(bf16[8,128,128]{2,1,0:T(8,128)(2,1)} %param.15) | copy-start | bytes 786436
  13.6 7.6 %copy-start.9 = (bf16[8,128,128]{2,1,0:T(8,128)(2,1)S(1)}, bf16[8,128,128]{2,1,0:T(8,128)(2,1)}, u32[]{:S(2)}) copy-start(bf16[8,128,128]{2,1,0:T(8,128)(2,1)} %param.16) | copy-start | bytes 786436
  13.6 56.0 %all-to-all-start = ((bf16[32,128,256]{2,1,0:T(8,128)(2,1)}), bf16[32,128,256]{2,1,0:T(8,128)(2,1)S(1)}, u32[]{:S(2)}, u32[]{:S(2)}) async-start(bf16[32,128,256]{2,1,0:T(8,128)(2,1)} %maximum_select_fusion), calls=%async_computation | async-start | bytes 4194304 | tf_op jit(solution)/shard_map/all_to_all | solution.py:490
  20.9 130.7 %all-gather.3.cloned.1.call-start = ((), (), s32[]{:S(2)}) async-start(), calls=%async_computation.1 | async-start | bytes 2506752 | tf_op jit(solution)/shard_map/all_gather | solution.py:530
  42.3 0.7 copy-start.5
  71.5 1.6 copy-start.3
  73.7 1.5 copy-start.6
  92.0 27.3 %copy-start.4 = (bf16[64,2048]{1,0:T(8,128)(2,1)S(1)}, bf16[64,2048]{1,0:T(8,128)(2,1)}, u32[]{:S(2)}) copy-start(bf16[64,2048]{1,0:T(8,128)(2,1)} %param.19) | copy-start | bytes 786436
  152.7 1.6 copy-start.2
  253.4 28.0 %copy-start.1 = (bf16[8,1024,128]{2,1,0:T(8,128)(2,1)S(1)}, bf16[8,1024,128]{2,1,0:T(8,128)(2,1)}, u32[]{:S(2)}) copy-start(bf16[8,1024,128]{2,1,0:T(8,128)(2,1)} %param.13) | copy-start | bytes 6291460
Sparse Core Ops, SparseCore 0:
  120.8 30.7 all-gather.2
